TPU v7x, 128 devices: a whole 4x4x4 slice. The times are simulated.
128 devices in a mesh: lon: 32 (over x_hi, z, y), ch: 4 (over x_lo, core).
Axes of the slice: x: 4 (x_hi: 2, x_lo: 2; x = x_hi * 2 + x_lo), y: 4, z: 4, core: 2. Of those that a mesh axis runs over, the one named last changes fastest.
Arguments:
- ocean_state: bfloat16 [400, 64, 4096], P('ch', None, 'lon'), may hold values from -6 to 6
- sea_mask: int32 [64, 4096], P(None, 'lon'), may hold values 0 or 1
- kernel: float32 [400, 49], P('ch'), may hold values from -0.875 to 0.875
- conv_bias: float32 [400], P('ch'), may hold values from -3 to 3
- norm_gain: float32 [400], replicated, may hold values from 0.1 to 1.9
- norm_bias: float32 [400], replicated, may hold values from -2 to 2
- weight_in: bfloat16 [400, 1600], replicated, may hold values from -0.3125 to 0.3125
- bias_in: float32 [1600], replicated, may hold values from -3 to 3
- weight_out: bfloat16 [1600, 400], replicated, may hold values from -0.15625 to 0.15625
- bias_out: float32 [400], replicated, may hold values from -3 to 3
- layer_scale: float32 [400], P('ch'), may hold values from 0.5 to 2
- cotangent: bfloat16 [400, 64, 4096], P('ch', None, 'lon'), may hold values from -6 to 6
Outputs:
- updated: bfloat16 [400, 64, 4096], P('ch', None, 'lon')
- grad_state: bfloat16 [400, 64, 4096], P('ch', None, 'lon')
- grad_weight_in: float32 [400, 1600], replicated
- grad_weight_out: float32 [1600, 400], replicated
Inputs may be any that keep to these rules, and one draw needn't show every extreme that they name: `sea_mask`: 1 marks an ocean cell, 0 a land cell.
All inputs are finite; a program needn't handle non-finite values. No bound on the sum of `sea_mask` on one device may be relied on, other than what follows from the above.
Results may differ from a plain program's by a relative error of at most 0.0077.
Values may be sent and summed in bfloat16 or wider, within the bound.
No kernel may reach another device: no remote copies, remote signals or barrier semaphores. Data moves between devices by JAX's collectives and lax.ppermute only.
A program may use at most 192 MiB of HBM per device.

v0:
```python
import math

import jax
import jax.numpy as jnp
from jax import lax
from jax.sharding import PartitionSpec as P

KW = 7


root_coef = math.sqrt(2.0 / math.pi)
cubic_coef = 0.044715
norm_eps = 1e-06


def extended(cells, sides, width):
    for axis, dim in sides:
        count = lax.axis_size(axis)
        head = lax.slice_in_dim(cells, 0, width, axis=dim)
        tail = lax.slice_in_dim(cells, cells.shape[dim] - width, cells.shape[dim], axis=dim)
        cells = jnp.concatenate(
            [
                lax.ppermute(tail, axis, [(i, (i + 1) % count) for i in range(count)]),
                cells,
                lax.ppermute(head, axis, [((i + 1) % count, i) for i in range(count)]),
            ],
            axis=dim,
        )
    return cells


def gelu_parts(pre_act):
    inner_arg = root_coef * (pre_act + cubic_coef * pre_act * pre_act * pre_act)
    tangent = jnp.tanh(inner_arg)
    gelu_value = 0.5 * pre_act * (1.0 + tangent)
    gelu_slope = 0.5 * (1.0 + tangent) + 0.5 * pre_act * (1.0 - tangent * tangent) * root_coef * (
        1.0 + 3.0 * cubic_coef * pre_act * pre_act
    )
    return (gelu_value, gelu_slope)


def depth_taps(padded, kernel, row_count, lon_cells):
    tap_total = jnp.zeros((padded.shape[0], row_count, lon_cells), jnp.float32)
    for row_off in range(KW):
        for col_off in range(KW):
            tap_total = (
                tap_total
                + kernel[:, row_off * KW + col_off][:, None, None]
                * padded[:, row_off : row_off + row_count, col_off : col_off + lon_cells]
            )
    return tap_total


def depth_back(padded_grad, kernel, row_count, lon_cells):
    span = KW - 1
    tap_total = jnp.zeros((padded_grad.shape[0], row_count, lon_cells), jnp.float32)
    for row_off in range(KW):
        for col_off in range(KW):
            tap_total = (
                tap_total
                + kernel[:, row_off * KW + col_off][:, None, None]
                * padded_grad[
                    :,
                    span - row_off : span - row_off + row_count,
                    span - col_off : span - col_off + lon_cells,
                ]
            )
    return tap_total


def block_math(
    conv_cells, grad_cells, norm_gain, norm_bias, weight_in, bias_in, weight_out, bias_out
):
    full_width = conv_cells.shape[0]
    values = conv_cells.astype(jnp.float32)
    mean_val = jnp.sum(values, axis=0) / full_width
    square = jnp.sum(values * values, axis=0) / full_width
    inv_std = lax.rsqrt(square - mean_val * mean_val + norm_eps)
    centred = (values - mean_val) * inv_std
    normed = (centred * norm_gain[:, None] + norm_bias[:, None]).astype(jnp.bfloat16)
    pre_act = jnp.dot(weight_in.T, normed, preferred_element_type=jnp.float32) + bias_in[:, None]
    gelu_value, gelu_slope = gelu_parts(pre_act)
    activation = gelu_value.astype(jnp.bfloat16)
    branch = (
        jnp.dot(weight_out.T, activation, preferred_element_type=jnp.float32) + bias_out[:, None]
    ).astype(jnp.bfloat16)
    grad_act = jnp.dot(weight_out, grad_cells, preferred_element_type=jnp.float32)
    grad_pre = (grad_act * gelu_slope).astype(jnp.bfloat16)
    part_out = jnp.dot(activation, grad_cells.T, preferred_element_type=jnp.float32)
    part_in = jnp.dot(normed, grad_pre.T, preferred_element_type=jnp.float32)
    grad_normed = jnp.dot(weight_in, grad_pre, preferred_element_type=jnp.float32)
    scaled_grad = grad_normed * norm_gain[:, None]
    mean_first = jnp.sum(scaled_grad, axis=0) / full_width
    mean_second = jnp.sum(scaled_grad * centred, axis=0) / full_width
    grad_conv = (inv_std * (scaled_grad - mean_first - centred * mean_second)).astype(jnp.bfloat16)
    return (branch, grad_conv, part_in, part_out)


def body(
    ocean_state,
    sea_mask,
    kernel,
    conv_bias,
    norm_gain,
    norm_bias,
    weight_in,
    bias_in,
    weight_out,
    bias_out,
    layer_scale,
    cotangent,
):
    local_chan, row_count, lon_cells = ocean_state.shape
    chan_groups = lax.axis_size("ch")
    full_width = local_chan * chan_groups
    rim_width = KW // 2
    grad_scale = 1.0 / math.sqrt(row_count * lon_cells * lax.axis_size("lon"))
    state_f = ocean_state.astype(jnp.float32)
    state_rim = extended(ocean_state, (("lon", 2),), rim_width)
    padded = jnp.pad(state_rim.astype(jnp.float32), ((0, 0), (rim_width, rim_width), (0, 0)))
    conv_out = (depth_taps(padded, kernel, row_count, lon_cells) + conv_bias[:, None, None]).astype(
        jnp.bfloat16
    )
    mask_f = sea_mask.astype(jnp.float32)[None]
    grad_out = cotangent.astype(jnp.float32) * mask_f
    grad_branch = (grad_out * layer_scale[:, None, None]).astype(jnp.bfloat16)
    quarter = row_count // chan_groups
    conv_cells, grad_cells = (
        lax.all_to_all(conv_out, "ch", split_axis=1, concat_axis=0, tiled=True),
        lax.all_to_all(grad_branch, "ch", split_axis=1, concat_axis=0, tiled=True),
    )
    branch_cells, conv_grad_cells, part_in, part_out = block_math(
        conv_cells.reshape(full_width, quarter * lon_cells),
        grad_cells.reshape(full_width, quarter * lon_cells),
        norm_gain,
        norm_bias,
        weight_in,
        bias_in,
        weight_out,
        bias_out,
    )
    branch, grad_conv = (
        lax.all_to_all(
            branch_cells.reshape(full_width, quarter, lon_cells),
            "ch",
            split_axis=0,
            concat_axis=1,
            tiled=True,
        ),
        lax.all_to_all(
            conv_grad_cells.reshape(full_width, quarter, lon_cells),
            "ch",
            split_axis=0,
            concat_axis=1,
            tiled=True,
        ),
    )
    sum_in, sum_out = lax.psum((part_in, part_out), ("lon", "ch"))
    grad_weight_in = sum_in * grad_scale
    grad_weight_out = sum_out * grad_scale
    updated = (mask_f * (state_f + layer_scale[:, None, None] * branch.astype(jnp.float32))).astype(
        jnp.bfloat16
    )
    grad_rim = extended(grad_conv, (("lon", 2),), rim_width)
    padded_grad = jnp.pad(grad_rim.astype(jnp.float32), ((0, 0), (rim_width, rim_width), (0, 0)))
    grad_state = (grad_out + depth_back(padded_grad, kernel, row_count, lon_cells)).astype(
        jnp.bfloat16
    )
    return (updated, grad_state, grad_weight_in, grad_weight_out)


def solution(mesh):
    return jax.shard_map(
        body,
        mesh=mesh,
        in_specs=(
            P("ch", None, "lon"),
            P(None, "lon"),
            P("ch", None),
            P("ch"),
            P(),
            P(),
            P(),
            P(),
            P(),
            P(),
            P("ch"),
            P("ch", None, "lon"),
        ),
        out_specs=(P("ch", None, "lon"), P("ch", None, "lon"), P(), P()),
        check_vma=False,
    )
```

profile of v0, /device:TPU:1, one launch (start us, length us, event | category | flops | bytes accessed | tf_op | source)
XLA Modules:
  0.0 416.4 jit_solution(18222858004938454714)
XLA Ops:
  7.2 4.5 %fusion.192 = (bf16[100,64,3]{2,1,0:T(8,128)(2,1)}, bf16[100,64,3]{2,1,0:T(8,128)(2,1)}) fusion(bf16[100,64,128]{2,1,0:T(8,128)(2,1)} %param.12), kind=kLoop, calls=%fused_computation.345 | loop fusion | bytes 153600 | tf_op jit(solution)/shard_map/slice | solution.py:20
  19.7 7.5 %collective-permute-start.1 = (bf16[100,64,3]{0,1,2:T(8,128)(2,1)S(1)}, bf16[100,64,3]{0,1,2:T(8,128)(2,1)S(1)}, u32[]{:S(2)}, u32[]{:S(2)}) collective-permute-start(bf16[100,64,3]{0,1,2:T(8,128)(2,1)S(1)} %copy.41), channel_id=1, source_target_pairs={{4,0},{8,4},{12,8},{16,12},{20,16},{24,20},{28,24},{32,28},{36,32}... | collective-permute-start | bytes 115208 | tf_op jit(solution)/shard_map/ppermute | solution.py:25
  33.7 4.3 %maximum_convert_fusion = f32[100,64,134]{2,0,1:T(8,128)S(1)} fusion(bf16[100,64,3]{2,0,1:T(8,128)(2,1)} %copy.28, bf16[100,64,128]{2,0,1:T(8,128)(2,1)} %copy.23, bf16[100,64,3]{2,0,1:T(8,128)(2,1)} %copy.26), kind=kLoop, calls=%fused_computation.82 | loop fusion | flops 5145600 | bytes 5145600 | tf_op jit(solution)/shard_map/convert_element_type | solution.py:120
  38.1 40.2 %add_convert_fusion = bf16[100,64,128]{2,0,1:T(8,128)(2,1)} fusion(f32[100,64,134]{2,0,1:T(8,128)S(1)} %maximum_convert_fusion, f32[100]{0:T(128)} %param.15, f32[100]{0:T(128)} %get-tuple-element.66, f32[100]{0:T(128)} %get-tuple-element.67, f32[100]{0:T(128)S(1)} %get-tuple-element.20, f32[100]{0:T(128)S(1)} %get-tuple-element.21, ...), kind=kLoop, calls=%fused_computation.176 | loop fusion | flops 81100800 | bytes 32333840 | tf_op jit(solution)/shard_map/convert_element_type | solution.py:121
  78.3 25.2 %all_to_all.51 = bf16[100,64,128]{2,0,1:T(8,128)(2,1)S(1)} all-to-all(bf16[100,64,128]{2,0,1:T(8,128)(2,1)} %add_convert_fusion), channel_id=1, replica_groups=mesh['lon'=32,'ch'=4] {'ch'}, dimensions={1} | all-to-all | bytes 3276800 | tf_op jit(solution)/shard_map/all_to_all | solution.py:129
  104.1 10.9 %multiply_convert_fusion = (bf16[1600,2048]{1,0:T(8,128)(2,1)S(1)}, f32[2048,1600]{0,1:T(8,128)}) fusion(f32[1600]{0:T(1024)S(1)} %copy-done.23, bf16[400,1600]{1,0:T(8,128)(2,1)S(1)} %copy-done, f32[50,8,16,128]{3,2,1,0:T(8,128)S(1)} %bitcast.202, f32[400]{0:T(512)S(1)} %copy-done.25, f32[400]{0:T(512)S(1)} %copy-done.26, f32[2048]{0:T(1024)S(1)} %fusion.188, ...), kind=kOutput, calls=%fused_computation.10 | convolution fusion | flops 2658304000 | bytes 24243584 | tf_op jit(solution)/shard_map/dot_general | solution.py:81
  115.0 3.2 fusion.184
  119.9 5.5 %all-to-all-start.1 = ((bf16[400,16,128]{2,1,0:T(8,128)(2,1)}), bf16[400,16,128]{2,1,0:T(8,128)(2,1)}, u32[]{:S(2)}, u32[]{:S(2)}) async-start(bf16[400,16,128]{2,1,0:T(8,128)(2,1)} %bitcast.209), calls=%async_computation.1 | async-start | bytes 3276800 | tf_op jit(solution)/shard_map/all_to_all | solution.py:143
  125.4 20.0 %all-to-all-done.1 = bf16[400,16,128]{2,1,0:T(8,128)(2,1)} async-done(((bf16[400,16,128]{2,1,0:T(8,128)(2,1)}), bf16[400,16,128]{2,1,0:T(8,128)(2,1)}, u32[]{:S(2)}, u32[]{:S(2)}) %all-to-all-start.1) | async-done | bytes 1638432 | tf_op jit(solution)/shard_map/all_to_all | solution.py:143
  147.3 3.6 multiply_convert_fusion.1
  150.9 24.1 %all_to_all.52 = bf16[100,64,128]{2,0,1:T(8,128)(2,1)S(1)} all-to-all(bf16[100,64,128]{2,0,1:T(8,128)(2,1)S(1)} %get-tuple-element.17), channel_id=1, replica_groups=mesh['lon'=32,'ch'=4] {'ch'}, dimensions={1} | all-to-all | bytes 3276800 | tf_op jit(solution)/shard_map/all_to_all | solution.py:130
  175.3 14.4 %fusion.6 = bf16[1600,2048]{1,0:T(8,128)(2,1)S(1)} fusion(f32[2048,1600]{0,1:T(8,128)} %get-tuple-element.69, bf16[1600,400]{0,1:T(8,128)(2,1)S(1)} %copy-done.22, f32[1600]{0:T(1024)S(1)} %copy-done.23, bf16[50,8,16,128]{3,2,1,0:T(8,128)(2,1)S(1)} %bitcast.210), kind=kOutput, calls=%fused_computation.8 | convolution fusion | flops 2686976000 | bytes 22585600 | tf_op jit(solution)/shard_map/dot_general | solution.py:87
  189.7 5.6 %fusion.178 = (f32[2048]{0:T(1024)S(1)}, f32[2048,400]{0,1:T(8,128)}) fusion(f32[50,8,16,128]{3,2,1,0:T(8,128)S(1)} %bitcast.205, f32[2048]{0:T(1024)S(1)} %fusion.188, f32[2048]{0:T(1024)S(1)} %multiply_bitcast_fusion, f32[400]{0:T(512)S(1)} %copy-done.26, bf16[400,1600]{1,0:T(8,128)(2,1)S(1)} %copy-done, bf16[1600,2048]{1,0:T(8,128)(2,1)S(1)} %fusion.6), kind=kOutput, calls=%fused_computation.271 | convolution fusion | flops 2625533952 | bytes 14413376 | tf_op jit(solution)/shard_map/dot_general | solution.py:91
  197.4 4.8 %fusion.180 = bf16[50,8,16,128]{3,1,2,0:T(8,128)(2,1)S(1)} fusion(f32[50,8,16,128]{3,2,1,0:T(8,128)} %bitcast.203, f32[2048,400]{0,1:T(8,128)} %get-tuple-element.71, f32[2048]{0:T(1024)S(1)} %get-tuple-element.72, f32[2048]{0:T(1024)S(1)} %get-tuple-element.73, f32[2048]{0:T(1024)S(1)} %fusion.188, f32[2048]{0:T(1024)S(1)} %multiply_bitcast_fusion), kind=kLoop, calls=%fused_computation.278 | loop fusion | flops 5734400 | bytes 8224768
  203.8 5.4 %all-to-all-start.3 = ((bf16[400,16,128]{2,1,0:T(8,128)(2,1)}), bf16[400,16,128]{2,1,0:T(8,128)(2,1)}, u32[]{:S(2)}, u32[]{:S(2)}) async-start(bf16[400,16,128]{2,1,0:T(8,128)(2,1)} %bitcast.208), calls=%async_computation.3 | async-start | bytes 3276800 | tf_op jit(solution)/shard_map/all_to_all | solution.py:150
  211.0 9.2 %fusion.189 = f32[400,1600]{1,0:T(8,128)} fusion(bf16[1600,2048]{1,0:T(8,128)(2,1)} %copy-done.27, f32[50,8,16,128]{3,2,1,0:T(8,128)} %bitcast.204, f32[400]{0:T(512)S(1)} %copy-done.25, f32[400]{0:T(512)S(1)} %copy-done.26, f32[2048]{0:T(1024)S(1)} %fusion.188, f32[2048]{0:T(1024)S(1)} %multiply_bitcast_fusion), kind=kOutput, calls=%fused_computation.342 | convolution fusion | flops 2625536000 | bytes 12409984 | tf_op jit(solution)/shard_map/dot_general | solution.py:90
  220.2 8.9 %all-to-all-done.3 = bf16[400,16,128]{2,1,0:T(8,128)(2,1)} async-done(((bf16[400,16,128]{2,1,0:T(8,128)(2,1)}), bf16[400,16,128]{2,1,0:T(8,128)(2,1)}, u32[]{:S(2)}, u32[]{:S(2)}) %all-to-all-start.3) | async-done | bytes 1638432 | tf_op jit(solution)/shard_map/all_to_all | solution.py:150
  235.8 7.5 %collective-permute-start.3 = (bf16[100,64,3]{0,1,2:T(8,128)(2,1)S(1)}, bf16[100,64,3]{0,1,2:T(8,128)(2,1)S(1)}, u32[]{:S(2)}, u32[]{:S(2)}) collective-permute-start(bf16[100,64,3]{0,1,2:T(8,128)(2,1)S(1)} %copy.35), channel_id=1, source_target_pairs={{4,0},{8,4},{12,8},{16,12},{20,16},{24,20},{28,24},{32,28},{36,32}... | collective-permute-start | bytes 115208 | tf_op jit(solution)/shard_map/ppermute | solution.py:25
  243.3 8.0 %fusion.181 = f32[1600,400]{0,1:T(8,128)} fusion(bf16[1600,2048]{1,0:T(8,128)(2,1)} %copy-done.28, bf16[50,8,16,128]{3,2,1,0:T(8,128)(2,1)} %bitcast.211), kind=kOutput, calls=%fused_computation.279 | convolution fusion | flops 2621440000 | bytes 10752000 | tf_op jit(solution)/shard_map/dot_general | solution.py:89
  255.0 4.7 %maximum_convert_fusion.1 = f32[100,64,134]{2,0,1:T(8,128)S(1)} fusion(bf16[100,64,3]{2,0,1:T(8,128)(2,1)} %copy.37, bf16[100,64,128]{2,0,1:T(8,128)(2,1)} %bitcast.201, bf16[100,64,3]{2,0,1:T(8,128)(2,1)} %copy.36), kind=kLoop, calls=%fused_computation.83 | loop fusion | flops 5145600 | bytes 5145600 | tf_op jit(solution)/shard_map/convert_element_type | solution.py:165
  259.7 41.0 %fusion.173 = bf16[100,64,128]{2,0,1:T(8,128)(2,1)} fusion(f32[100,64,134]{2,0,1:T(8,128)S(1)} %maximum_convert_fusion.1, f32[100]{0:T(128)} %get-tuple-element.66, f32[100]{0:T(128)} %get-tuple-element.67, f32[100]{0:T(128)S(1)} %get-tuple-element.20, f32[100]{0:T(128)S(1)} %get-tuple-element.21, f32[100]{0:T(128)S(1)} %get-tuple-element.22, ...), kind=kLoop, calls=%fused_computation.263 | loop fusion | flops 82739200 | bytes 34003712 | tf_op jit(solution)/shard_map/convert_element_type | solution.py:166
  300.7 3.1 copy.39
  303.8 100.0 %all-reduce.5.cloned.1.call-done = (f32[400,1600]{1,0:T(8,128)}, f32[1600,400]{0,1:T(8,128)}) async-done(((f32[400,1600]{1,0:T(8,128)}, f32[1600,400]{0,1:T(8,128)}), (f32[400,1600]{1,0:T(8,128)}, f32[1600,400]{0,1:T(8,128)})) %all-reduce.5.cloned.1.call-update) | async-done | bytes 5120016 | tf_op jit(solution)/shard_map/psum | solution.py:158
  403.8 3.6 broadcast_multiply_fusion
  (92 shorter events, 36.3 us)
Async XLA Ops:
  7.2 96.8 %copy-start = (bf16[400,1600]{1,0:T(8,128)(2,1)S(1)}, bf16[400,1600]{1,0:T(8,128)(2,1)}, u32[]{:S(2)}) copy-start(bf16[400,1600]{1,0:T(8,128)(2,1)} %param.18) | copy-start | bytes 3840004
  7.2 20.6 %copy-start.2 = (bf16[100,64,128]{2,1,0:T(8,128)(2,1)S(1)}, bf16[100,64,128]{2,1,0:T(8,128)(2,1)}, u32[]{:S(2)}) copy-start(bf16[100,64,128]{2,1,0:T(8,128)(2,1)} %param.12) | copy-start | bytes 4915204
  7.2 19.9 %copy-start.11 = (f32[100,49]{0,1:T(8,128)S(1)}, f32[100,49]{0,1:T(8,128)}, u32[]{:S(2)}) copy-start(f32[100,49]{0,1:T(8,128)} %param.14) | copy-start | bytes 58804
  14.6 15.5 %collective-permute-start = (bf16[100,64,3]{0,1,2:T(8,128)(2,1)S(1)}, bf16[100,64,3]{0,1,2:T(8,128)(2,1)S(1)}, u32[]{:S(2)}, u32[]{:S(2)}) collective-permute-start(bf16[100,64,3]{0,1,2:T(8,128)(2,1)S(1)} %copy.40), channel_id=1, source_target_pairs={{0,4},{4,8},{8,12},{12,16},{16,20},{20,24},{24,28},{28,32},{32,36}... | collective-permute-start | bytes 115208 | tf_op jit(solution)/shard_map/ppermute | solution.py:23
  19.7 12.2 %collective-permute-start.1 = (bf16[100,64,3]{0,1,2:T(8,128)(2,1)S(1)}, bf16[100,64,3]{0,1,2:T(8,128)(2,1)S(1)}, u32[]{:S(2)}, u32[]{:S(2)}) collective-permute-start(bf16[100,64,3]{0,1,2:T(8,128)(2,1)S(1)} %copy.41), channel_id=1, source_target_pairs={{4,0},{8,4},{12,8},{16,12},{20,16},{24,20},{28,24},{32,28},{36,32}... | collective-permute-start | bytes 115208 | tf_op jit(solution)/shard_map/ppermute | solution.py:25
  27.2 10.8 %copy-start.12 = (f32[100]{0:T(128)}, f32[100]{0:T(128)S(1)}, u32[]{:S(2)}) copy-start(f32[100]{0:T(128)S(1)} %get-tuple-element.52) | copy-start | bytes 1204
  27.2 10.8 %copy-start.13 = (f32[100]{0:T(128)}, f32[100]{0:T(128)S(1)}, u32[]{:S(2)}) copy-start(f32[100]{0:T(128)S(1)} %get-tuple-element.53) | copy-start | bytes 1204
  27.2 10.8 %copy-start.14 = (f32[100]{0:T(128)}, f32[100]{0:T(128)S(1)}, u32[]{:S(2)}) copy-start(f32[100]{0:T(128)S(1)} %get-tuple-element.54) | copy-start | bytes 1204
  78.2 25.8 %copy-start.23 = (f32[1600]{0:T(1024)S(1)}, f32[1600]{0:T(1024)}, u32[]{:S(2)}) copy-start(f32[1600]{0:T(1024)} %param.19) | copy-start | bytes 19204
  78.2 25.8 %copy-start.25 = (f32[400]{0:T(512)S(1)}, f32[400]{0:T(512)}, u32[]{:S(2)}) copy-start(f32[400]{0:T(512)} %param.17) | copy-start | bytes 4804
  78.3 25.8 %copy-start.26 = (f32[400]{0:T(512)S(1)}, f32[400]{0:T(512)}, u32[]{:S(2)}) copy-start(f32[400]{0:T(512)} %param.16) | copy-start | bytes 4804
  104.0 11.0 %copy-start.4 = (f32[100,4,16,128]{3,2,0,1:T(8,128)}, f32[100,4,16,128]{3,2,0,1:T(8,128)S(1)}, u32[]{:S(2)}) copy-start(f32[100,4,16,128]{3,2,0,1:T(8,128)S(1)} %get-tuple-element.12) | copy-start | bytes 9830404
  104.0 11.0 %copy-start.21 = (bf16[1600,400]{0,1:T(8,128)(2,1)S(1)}, bf16[1600,400]{0,1:T(8,128)(2,1)}, u32[]{:S(2)}) copy-start(bf16[1600,400]{0,1:T(8,128)(2,1)} %param.20) | copy-start | bytes 3840004
  104.1 11.0 %copy-start.24 = (f32[400]{0:T(512)S(1)}, f32[400]{0:T(512)}, u32[]{:S(2)}) copy-start(f32[400]{0:T(512)} %param.21) | copy-start | bytes 4804
  119.9 27.4 %copy-start.3 = (bf16[100,64,128]{2,1,0:T(8,128)(2,1)S(1)}, bf16[100,64,128]{2,1,0:T(8,128)(2,1)}, u32[]{:S(2)}) copy-start(bf16[100,64,128]{2,1,0:T(8,128)(2,1)} %param.12) | copy-start | bytes 4915204
  119.9 27.4 %copy-start.20 = (f32[100]{0:T(128)S(1)}, f32[100]{0:T(128)}, u32[]{:S(2)}) copy-start(f32[100]{0:T(128)} %param.22) | copy-start | bytes 1204
  119.9 25.5 %all-to-all-start.1 = ((bf16[400,16,128]{2,1,0:T(8,128)(2,1)}), bf16[400,16,128]{2,1,0:T(8,128)(2,1)}, u32[]{:S(2)}, u32[]{:S(2)}) async-start(bf16[400,16,128]{2,1,0:T(8,128)(2,1)} %bitcast.209), calls=%async_computation.1 | async-start | bytes 3276800 | tf_op jit(solution)/shard_map/all_to_all | solution.py:143
  150.9 24.3 %copy-start.22 = (bf16[1600,400]{0,1:T(8,128)(2,1)S(1)}, bf16[1600,400]{0,1:T(8,128)(2,1)}, u32[]{:S(2)}) copy-start(bf16[1600,400]{0,1:T(8,128)(2,1)} %param.20) | copy-start | bytes 3840004
  175.2 14.4 %copy-start.9 = (bf16[100,4,16,128]{3,2,0,1:T(8,128)(2,1)}, bf16[100,4,16,128]{3,2,0,1:T(8,128)(2,1)S(1)}, u32[]{:S(2)}) copy-start(bf16[100,4,16,128]{3,2,0,1:T(8,128)(2,1)S(1)} %copy.32) | copy-start | bytes 4915204
  175.2 14.4 %copy-start.5 = (f32[100,4,16,128]{3,2,0,1:T(8,128)S(1)}, f32[100,4,16,128]{3,2,0,1:T(8,128)}, u32[]{:S(2)}) copy-start(f32[100,4,16,128]{3,2,0,1:T(8,128)} %copy-done.4) | copy-start | bytes 9830404
  203.8 25.4 %all-to-all-start.3 = ((bf16[400,16,128]{2,1,0:T(8,128)(2,1)}), bf16[400,16,128]{2,1,0:T(8,128)(2,1)}, u32[]{:S(2)}, u32[]{:S(2)}) async-start(bf16[400,16,128]{2,1,0:T(8,128)(2,1)} %bitcast.208), calls=%async_computation.3 | async-start | bytes 3276800 | tf_op jit(solution)/shard_map/all_to_all | solution.py:150
  209.1 194.7 %all-reduce.5.cloned.1.call-start = ((), (), s32[]{:S(2)}) async-start(), calls=%async_computation.4 | async-start | bytes 10649600 | tf_op jit(solution)/shard_map/psum | solution.py:158
  234.8 16.5 %collective-permute-start.2 = (bf16[100,64,3]{0,1,2:T(8,128)(2,1)S(1)}, bf16[100,64,3]{0,1,2:T(8,128)(2,1)S(1)}, u32[]{:S(2)}, u32[]{:S(2)}) collective-permute-start(bf16[100,64,3]{0,1,2:T(8,128)(2,1)S(1)} %copy.34), channel_id=1, source_target_pairs={{0,4},{4,8},{8,12},{12,16},{16,20},{20,24},{24,28},{28,32},{32,36}... | collective-permute-start | bytes 115208 | tf_op jit(solution)/shard_map/ppermute | solution.py:23
  235.8 17.4 %collective-permute-start.3 = (bf16[100,64,3]{0,1,2:T(8,128)(2,1)S(1)}, bf16[100,64,3]{0,1,2:T(8,128)(2,1)S(1)}, u32[]{:S(2)}, u32[]{:S(2)}) collective-permute-start(bf16[100,64,3]{0,1,2:T(8,128)(2,1)S(1)} %copy.35), channel_id=1, source_target_pairs={{4,0},{8,4},{12,8},{16,12},{20,16},{24,20},{28,24},{32,28},{36,32}... | collective-permute-start | bytes 115208 | tf_op jit(solution)/shard_map/ppermute | solution.py:25
  (12 other events, 82.8 us)
Sparse Core Ops, SparseCore 0:
  251.4 152.3 all-reduce.4
where the time goes:
time: 424 us; the launch traced here: 416 us
  waiting for transfers between devices  129 us (30%)
  other arithmetic  106 us (25%)
  matrix products  51.3 us (12%)
  blocking collectives  49.3 us (12%)
  local copies, waits for them, and re-layouts  37 us (9%)
  starting transfers between devices  28.4 us (7%)
  between operations  15 us (4%)
    psum x1, waiting for transfers between devices, body(): sum_in, sum_out = lax.psum((part_in, part_out), ('lon', 'ch'))  100 us
    convert_element_type x1, other arithmetic, body(): (grad_out + depth_back(padded_grad, kernel, row_count, lon_cells)).astype...  41 us
    convert_element_type x1, other arithmetic, body(): (depth_taps(padded, kernel, row_count, lon_cells) + conv_bias[:, None, No...  40.2 us
    all_to_all x1, blocking collectives, body(): lax.all_to_all(conv_out, 'ch', split_axis=1, concat_axis=0, tiled=True)  25.2 us
    all_to_all x1, blocking collectives, body(): lax.all_to_all(grad_branch, 'ch', split_axis=1, concat_axis=0, tiled=True)  24.1 us
    all_to_all x1, waiting for transfers between devices, body(): lax.all_to_all(branch_cells.reshape(full_width, quarter, lon_cells), 'ch'...  20 us
    unnamed x65, local copies, waits for them, and re-layouts  16.1 us
    ppermute x2, starting transfers between devices, extended(): lax.ppermute(head, axis, [((i + 1) % count, i) for i in range(count)])  15 us
  transfers between devices with their start and end apart: 7, of which 3 were waited for; matrix products, arithmetic and copies ran while one was open for 19% of the time, Pallas kernels for 0%

commit v1 on v0

v1 whole, which is shorter than its diff:
```python
import math

import jax
import jax.numpy as jnp
from jax import lax
from jax.experimental import pallas as pl
from jax.experimental.pallas import tpu as pltpu
from jax.sharding import PartitionSpec as P

KW = 7
RIM = KW // 2
C = 400
HID = 1600
ROWS = 64
LANES = 128
LC = 100
CP = 104
QR = 16
GROUP = 8
BF = jnp.bfloat16
F32 = jnp.float32

root_coef = math.sqrt(2.0 / math.pi)
cubic_coef = 0.044715
norm_eps = 1e-06


def dotg(a, b, ca, cb):
    return lax.dot_general(a, b, (((ca,), (cb,)), ((), ())), preferred_element_type=F32)


def ch_swap(x, k):
    return lax.ppermute(x, "ch", [(i, i ^ k) for i in range(4)])


def lon_shift(x, d):
    return lax.ppermute(x, "lon", [(i, (i + d) % 32) for i in range(32)])


def lon_swap(x, k):
    return lax.ppermute(x, "lon", [(i, i ^ k) for i in range(32)])


def share_kernel(me_ref, cot_ref, mask_ref, scale_ref, out_ref):
    cells = cot_ref[...].astype(F32)
    cells = jnp.concatenate([cells, jnp.zeros((CP - LC, QR, LANES), F32)], axis=0)
    cells = jnp.swapaxes(cells, 0, 1)
    mask = mask_ref[...].astype(F32)
    out_ref[...] = ((cells * mask[:, None, :]) * scale_ref[...][None]).astype(BF)


def branch_share(me, cotangent, sea_mask, scale, k):
    return pl.pallas_call(
        share_kernel,
        out_shape=jax.ShapeDtypeStruct((QR, CP, LANES), BF),
        grid_spec=pltpu.PrefetchScalarGridSpec(
            num_scalar_prefetch=1,
            grid=(1,),
            in_specs=[
                pl.BlockSpec((LC, QR, LANES), lambda i, me: (0, me[0] ^ k, 0)),
                pl.BlockSpec((QR, LANES), lambda i, me: (me[0] ^ k, 0)),
                pl.BlockSpec((CP, 1), lambda i, me: (0, 0)),
            ],
            out_specs=pl.BlockSpec((QR, CP, LANES), lambda i, me: (0, 0, 0)),
        ),
        compiler_params=pltpu.CompilerParams(vmem_limit_bytes=32 << 20),
        name="branch_share",
    )(me, cotangent, sea_mask, scale)


def conv_channel(cells, rim, pattern, lane, band):
    moved = []
    for off in range(-RIM, RIM + 1):
        if off == 0:
            moved.append(cells.astype(BF))
        else:
            edge = lane < off if off > 0 else lane >= LANES + off
            moved.append(pltpu.roll(jnp.where(edge, rim, cells), (-off) % LANES, 1).astype(BF))
    stacked = jnp.concatenate(moved, axis=0)
    tiles = []
    for t in range(4):
        row = jnp.broadcast_to(pattern[t : t + 1, :], (ROWS, LANES))
        row = pltpu.roll(row, 0, 1, stride=1, stride_axis=0)
        tiles.append(jnp.where(band, row, 0.0).astype(BF))
    banded = jnp.concatenate(tiles, axis=1)[:, : KW * ROWS]
    return jnp.dot(banded, stacked, preferred_element_type=F32)


def masks():
    lane = lax.broadcasted_iota(jnp.int32, (ROWS, LANES), 1)
    row = lax.broadcasted_iota(jnp.int32, (ROWS, LANES), 0)
    away = (lane & (ROWS - 1)) - row
    return lane, (away >= -RIM) & (away <= RIM)


def forward_kernel(me_ref, state_ref, rim_ref, pat_ref, bias_ref, o0, o1, o2, o3, held):
    step = pl.program_id(0)
    lane, band = masks()
    outs = []
    for c in range(GROUP):
        total = conv_channel(
            state_ref[c].astype(F32), rim_ref[c].astype(F32), pat_ref[c], lane, band
        )
        total = total + bias_ref[c]
        outs.append(jnp.where(step * GROUP + c < LC, total, 0.0))
    held[...] = jnp.swapaxes(jnp.stack(outs, 0), 0, 1).reshape(4, QR, GROUP, LANES)
    me = me_ref[0]
    for k, out in enumerate((o0, o1, o2, o3)):
        out[...] = held[me ^ k].astype(BF)


def conv_forward(me, state, rim, pattern, bias):
    share = jax.ShapeDtypeStruct((QR, CP, LANES), BF)
    return pl.pallas_call(
        forward_kernel,
        out_shape=[share] * 4,
        grid_spec=pltpu.PrefetchScalarGridSpec(
            num_scalar_prefetch=1,
            grid=(CP // GROUP,),
            in_specs=[
                pl.BlockSpec((GROUP, ROWS, LANES), lambda i, me: (i, 0, 0)),
                pl.BlockSpec((GROUP, ROWS, LANES), lambda i, me: (i, 0, 0)),
                pl.BlockSpec((GROUP, 4, LANES), lambda i, me: (i, 0, 0)),
                pl.BlockSpec((GROUP, 1, LANES), lambda i, me: (i, 0, 0)),
            ],
            out_specs=[pl.BlockSpec((QR, GROUP, LANES), lambda i, me: (0, i, 0))] * 4,
            scratch_shapes=[pltpu.VMEM((4, QR, GROUP, LANES), F32)],
        ),
        compiler_params=pltpu.CompilerParams(vmem_limit_bytes=32 << 20),
        name="conv_forward",
    )(me, state, rim, pattern, bias)


def backward_kernel(
    me_ref, g0, g1, g2, g3, r0, r1, r2, r3, pat_ref, cot_ref, mask_ref, out_ref, held, held_rim
):
    lane, band = masks()
    me = me_ref[0]
    for k, (cells, rim) in enumerate(((g0, r0), (g1, r1), (g2, r2), (g3, r3))):
        held[me ^ k] = cells[...].astype(F32)
        held_rim[me ^ k] = rim[...].astype(F32)
    cells = jnp.swapaxes(held[...].reshape(ROWS, GROUP, LANES), 0, 1)
    rims = jnp.swapaxes(held_rim[...].reshape(ROWS, GROUP, LANES), 0, 1)
    mask = mask_ref[...].astype(F32)
    for c in range(GROUP):
        total = conv_channel(cells[c], rims[c], pat_ref[c], lane, band)
        out_ref[c] = (cot_ref[c].astype(F32) * mask + total).astype(BF)


def conv_backward(me, grads, rims, pattern, cotangent, sea_mask):
    piece = pl.BlockSpec((QR, GROUP, LANES), lambda i, me: (0, i, 0))
    return pl.pallas_call(
        backward_kernel,
        out_shape=jax.ShapeDtypeStruct((LC, ROWS, LANES), BF),
        grid_spec=pltpu.PrefetchScalarGridSpec(
            num_scalar_prefetch=1,
            grid=(CP // GROUP,),
            in_specs=[piece] * 8
            + [
                pl.BlockSpec((GROUP, 4, LANES), lambda i, me: (i, 0, 0)),
                pl.BlockSpec((GROUP, ROWS, LANES), lambda i, me: (i, 0, 0)),
                pl.BlockSpec((ROWS, LANES), lambda i, me: (0, 0)),
            ],
            out_specs=pl.BlockSpec((GROUP, ROWS, LANES), lambda i, me: (i, 0, 0)),
            scratch_shapes=[pltpu.VMEM((4, QR, GROUP, LANES), F32)] * 2,
        ),
        compiler_params=pltpu.CompilerParams(vmem_limit_bytes=32 << 20),
        name="conv_backward",
    )(me, *grads, *rims, pattern, cotangent, sea_mask)


CHUNK = 4
CELLS = CHUNK * LANES
HT = 400


def mlp_kernel(*refs):
    me_ref, core_ref = refs[:2]
    xs, gs = refs[2:6], refs[6:10]
    win_t, win, wout, wout_t, vec, bias_in = refs[10:16]
    brs, gcs = refs[16:20], refs[20:24]
    wgrad = refs[24]
    x_all, g_all, act, gpre, sum_in, sum_out = refs[25:]
    step = pl.program_id(0)
    me = me_ref[0]
    for k in range(4):
        x = xs[k][...]
        g = gs[k][...]
        for r in range(CHUNK):
            x_all[me ^ k, :, r * LANES : (r + 1) * LANES] = x[r].astype(F32)
            g_all[me ^ k, :, r * LANES : (r + 1) * LANES] = g[r].astype(F32)
    gain = vec[:, 0:1]
    values = x_all[...].reshape(4 * CP, CELLS)
    mean_val = jnp.sum(values, axis=0, keepdims=True) / C
    square = jnp.sum(values * values, axis=0, keepdims=True) / C
    inv_std = lax.rsqrt(square - mean_val * mean_val + norm_eps)
    normed = ((values - mean_val) * inv_std * gain + vec[:, 1:2]).astype(BF)
    grads = g_all[...].reshape(4 * CP, CELLS).astype(BF)
    for t in range(HID // HT):
        rows = slice(t * HT, (t + 1) * HT)
        pre = jnp.dot(win_t[rows, :], normed, preferred_element_type=F32) + bias_in[rows, :]
        gact = jnp.dot(wout[rows, :], grads, preferred_element_type=F32)
        sq = pre * pre
        tangent = jnp.tanh(pre * (root_coef + (root_coef * cubic_coef) * sq))
        half = 0.5 + 0.5 * tangent
        value = pre * half
        slope = half + value * (1.0 - half) * (
            2.0 * root_coef + (6.0 * root_coef * cubic_coef) * sq
        )
        act[rows, :] = value.astype(BF)
        gpre[rows, :] = (gact * slope).astype(BF)
    branch = jnp.dot(wout_t[...], act[...], preferred_element_type=F32) + vec[:, 2:3]
    x_grad = jnp.dot(win[...], gpre[...], preferred_element_type=F32) * gain
    centred = (x_all[...].reshape(4 * CP, CELLS) - mean_val) * inv_std
    first = jnp.sum(x_grad, axis=0, keepdims=True) / C
    second = jnp.sum(x_grad * centred, axis=0, keepdims=True) / C
    x_grad = inv_std * (x_grad - first - centred * second)
    x_all[...] = x_grad.reshape(4, CP, CELLS)
    g_all[...] = branch.reshape(4, CP, CELLS)
    for k in range(4):
        for r in range(CHUNK):
            gcs[k][r] = x_all[me ^ k, :, r * LANES : (r + 1) * LANES].astype(BF)
            brs[k][r] = g_all[me ^ k, :, r * LANES : (r + 1) * LANES].astype(BF)
    part_in = dotg(gpre[...], normed, 1, 1)
    part_out = dotg(act[...], grads, 1, 1)

    @pl.when(step == 0)
    def _():
        sum_in[...] = part_in
        sum_out[...] = part_out

    @pl.when(step > 0)
    def _():
        sum_in[...] += part_in
        sum_out[...] += part_out

    @pl.when(step == pl.num_programs(0) - 1)
    def _():
        core = core_ref[0]
        wgrad[core] = sum_in[...].astype(BF)
        wgrad[1 - core] = sum_out[...].astype(BF)


def mlp(me, core, xs, gs, weights, vec, bias_in):
    piece = pl.BlockSpec((CHUNK, CP, LANES), lambda i, me, core: (i, 0, 0))

    def whole(shape):
        return pl.BlockSpec(
            shape, lambda i, me, core: (0,) * len(shape), pipeline_mode=pl.Buffered(1)
        )

    share = jax.ShapeDtypeStruct((QR, CP, LANES), BF)
    outs = pl.pallas_call(
        mlp_kernel,
        out_shape=[share] * 8 + [jax.ShapeDtypeStruct((2, HID, 4 * CP), BF)],
        grid_spec=pltpu.PrefetchScalarGridSpec(
            num_scalar_prefetch=2,
            grid=(QR // CHUNK,),
            in_specs=[piece] * 8
            + [
                whole((HID, 4 * CP)),
                whole((4 * CP, HID)),
                whole((HID, 4 * CP)),
                whole((4 * CP, HID)),
                whole((4 * CP, 3)),
                whole((HID, 1)),
            ],
            out_specs=[piece] * 8 + [whole((2, HID, 4 * CP))],
            scratch_shapes=[
                pltpu.VMEM((4, CP, CELLS), F32),
                pltpu.VMEM((4, CP, CELLS), F32),
                pltpu.VMEM((HID, CELLS), BF),
                pltpu.VMEM((HID, CELLS), BF),
                pltpu.VMEM((HID, 4 * CP), F32),
                pltpu.VMEM((HID, 4 * CP), F32),
            ],
        ),
        compiler_params=pltpu.CompilerParams(vmem_limit_bytes=56 << 20),
        name="mlp",
    )(me, core, *xs, *gs, *weights, vec, bias_in)
    return outs[:4], outs[4:8], outs[8]


def update_kernel(me_ref, b0, b1, b2, b3, state_ref, mask_ref, scale_ref, out_ref):
    k = pl.program_id(0)

    def write(piece):
        branch = piece[...].astype(F32) * scale_ref[...][None]
        branch = jnp.swapaxes(branch, 0, 1)[:LC]
        mask = mask_ref[...].astype(F32)
        out_ref[...] = (mask[None] * (state_ref[...].astype(F32) + branch)).astype(BF)

    for i, piece in enumerate((b0, b1, b2, b3)):
        pl.when(k == i)(lambda piece=piece: write(piece))


def update(me, pieces, state, sea_mask, scale):
    whole = pl.BlockSpec((QR, CP, LANES), lambda i, me: (0, 0, 0), pipeline_mode=pl.Buffered(1))
    return pl.pallas_call(
        update_kernel,
        out_shape=jax.ShapeDtypeStruct((LC, ROWS, LANES), BF),
        grid_spec=pltpu.PrefetchScalarGridSpec(
            num_scalar_prefetch=1,
            grid=(4,),
            in_specs=[whole] * 4
            + [
                pl.BlockSpec((LC, QR, LANES), lambda i, me: (0, me[0] ^ i, 0)),
                pl.BlockSpec((QR, LANES), lambda i, me: (me[0] ^ i, 0)),
                pl.BlockSpec((CP, 1), lambda i, me: (0, 0)),
            ],
            out_specs=pl.BlockSpec((LC, QR, LANES), lambda i, me: (0, me[0] ^ i, 0)),
        ),
        compiler_params=pltpu.CompilerParams(vmem_limit_bytes=32 << 20),
        name="update",
    )(me, *pieces, state, sea_mask, scale)


def tap_patterns(kernel):
    lane = jnp.arange(4 * LANES)
    tile, pos = lane // LANES, lane % LANES
    away = jnp.where(pos % ROWS < ROWS // 2, pos % ROWS, pos % ROWS - ROWS)
    side = ((pos - away) // ROWS) % 2
    col = 2 * tile + side
    tap = jnp.where((jnp.abs(away) <= RIM) & (col < KW), (away + RIM) * KW + col, -1)
    pick = (jnp.arange(KW * KW)[:, None] == tap[None, :]).astype(BF)
    return jnp.dot(kernel.astype(BF), pick, preferred_element_type=F32).reshape(LC, 4, LANES)


def edge_picks():
    row = jnp.arange(8)[:, None]
    lane = jnp.arange(LANES)[None, :]
    head = ((row < RIM) & (lane == row)).astype(BF)
    tail = ((row < RIM) & (lane == LANES - RIM + row)).astype(BF)
    return head, tail


def rims(cells2d):
    head, tail = edge_picks()
    first = dotg(head, cells2d, 1, 1).astype(BF)
    last = dotg(tail, cells2d, 1, 1).astype(BF)
    from_right = lon_shift(first, -1)
    from_left = lon_shift(last, 1)
    return dotg(
        jnp.concatenate([from_right, from_left], 0), jnp.concatenate([head, tail], 0), 0, 0
    ).astype(BF)


def reduce_gradients(wgrad, lon):
    y, z = lon & 3, (lon >> 2) & 3
    mine = wgrad[0].astype(F32) + ch_swap(wgrad[1], 1).astype(F32)
    mine = mine.reshape(4, HID // 4, 4 * CP)
    wire = mine.astype(BF)
    total = lax.dynamic_index_in_dim(mine, y, 0, False)
    for k in (1, 2, 3):
        total = total + lon_swap(
            lax.dynamic_index_in_dim(wire, y ^ k, 0, False), k
        ).astype(F32)

    def strip(a, i):
        return lax.dynamic_slice_in_dim(a, jnp.minimum(i * 104, 296), 104, 0)

    wire = total.astype(BF)
    part = strip(total, z)
    for k in (1, 2, 3):
        part = part + lon_swap(strip(wire, z ^ k), 4 * k).astype(F32)
    wire = part.astype(BF)
    part = (
        (wire.astype(F32) + lon_swap(wire, 16).astype(F32))
        + (ch_swap(wire, 2).astype(F32) + both_swap(wire).astype(F32))
    ).astype(BF)
    others = [part] + [lon_swap(part, 4 * k) for k in (1, 2, 3)]
    strips = jnp.stack(others)
    block = jnp.zeros((HID // 4, 4 * CP), BF)
    for k in range(4):
        block = lax.dynamic_update_slice_in_dim(
            block,
            lax.dynamic_index_in_dim(strips, z ^ k, 0, False),
            min(k * 104, 296),
            0,
        )
    blocks = jnp.stack([block] + [lon_swap(block, k) for k in (1, 2, 3)])
    full = jnp.concatenate([lax.dynamic_index_in_dim(blocks, y ^ k, 0, False) for k in range(4)], 0)
    return full, ch_swap(full, 1)


def both_swap(x):
    return lax.ppermute(x, ("lon", "ch"), [(i, i ^ (16 * 4 + 2)) for i in range(128)])


def body(
    ocean_state,
    sea_mask,
    kernel,
    conv_bias,
    norm_gain,
    norm_bias,
    weight_in,
    bias_in,
    weight_out,
    bias_out,
    layer_scale,
    cotangent,
):
    ch = lax.axis_index("ch")
    lon = lax.axis_index("lon")
    me = ch.reshape(1)
    core = (ch & 1).reshape(1)
    scale = jnp.pad(layer_scale, (0, CP - LC)).reshape(CP, 1)

    sent = {k: branch_share(me, cotangent, sea_mask, scale, k) for k in (2, 3, 1, 0)}
    gs = [sent[0]] + [ch_swap(sent[k], k) for k in (1, 2, 3)]

    chan = jnp.arange(C)
    pad = ((chan // LC * CP + chan % LC)[:, None] == jnp.arange(4 * CP)[None, :]).astype(BF)
    win = dotg(pad, weight_in, 0, 0).astype(BF)
    win_t = dotg(weight_in, pad, 0, 0).astype(BF)
    wout = dotg(weight_out, pad, 1, 0).astype(BF)
    wout_t = dotg(pad, weight_out, 0, 1).astype(BF)
    vec = jnp.stack([norm_gain, norm_bias, bias_out], 1).reshape(4, LC, 3)
    vec = jnp.pad(vec, ((0, 0), (0, CP - LC), (0, 0))).reshape(4 * CP, 3)

    state_rim = rims(ocean_state.reshape(LC * ROWS, LANES)).reshape(LC, ROWS, LANES)
    bias = jnp.broadcast_to(conv_bias[:, None, None], (LC, 1, LANES))
    conv = conv_forward(me, ocean_state, state_rim, tap_patterns(kernel), bias)
    xs = [conv[0]] + [ch_swap(conv[k], k) for k in (1, 2, 3)]

    branch, grad, wgrad = mlp(
        me, core, xs, gs, (win_t, win, wout, wout_t), vec, bias_in.reshape(HID, 1)
    )

    grads = [grad[0]] + [ch_swap(grad[k], k) for k in (1, 2, 3)]
    pieces = [branch[0]] + [ch_swap(branch[k], k) for k in (1, 2, 3)]

    every = jnp.concatenate(grads, 0).reshape(4 * QR * CP, LANES)
    grad_rims = rims(every).reshape(4, QR, CP, LANES)
    grad_state = conv_backward(
        me,
        grads,
        [grad_rims[k] for k in range(4)],
        tap_patterns(kernel[:, ::-1]),
        cotangent,
        sea_mask,
    )
    updated = update(me, pieces, ocean_state, sea_mask, scale)

    full, other = reduce_gradients(wgrad, lon)
    first = (ch & 1) == 0
    grad_in = jnp.where(first, full, other)
    grad_out = jnp.where(first, other, full)
    grad_scale = 1.0 / math.sqrt(ROWS * LANES * lax.axis_size("lon"))
    return (
        updated,
        grad_state,
        dotg(pad, grad_in, 1, 1) * grad_scale,
        dotg(grad_out, pad, 1, 1) * grad_scale,
    )


def solution(mesh):
    return jax.shard_map(
        body,
        mesh=mesh,
        in_specs=(
            P("ch", None, "lon"),
            P(None, "lon"),
            P("ch", None),
            P("ch"),
            P(),
            P(),
            P(),
            P(),
            P(),
            P(),
            P("ch"),
            P("ch", None, "lon"),
        ),
        out_specs=(P("ch", None, "lon"), P("ch", None, "lon"), P(), P()),
        check_vma=False,
    )
```

time: 424 us -> 243 us (0.57); the launches traced: 416 us -> 242 us
  other arithmetic: 106 us -> 7.51 us
  waiting for transfers between devices: 129 us -> 44.2 us
  Pallas kernels: 0 us -> 61.8 us
  blocking collectives: 49.3 us -> 0 us
  matrix products: 51.3 us -> 23 us
  starting transfers between devices: 28.4 us -> 56.6 us
  between operations: 15 us -> 0.99 us
  local copies, waits for them, and re-layouts: 37 us -> 48.2 us
    psum x1 -> x0, waiting for transfers between devices: 100 us -> none  [body(): sum_in, sum_out = lax.psum((part_in, part_out), ('lon', 'ch'))]
    convert_element_type x6 -> x4, other arithmetic: 93.8 us -> 1.98 us  [the longest x1 1.62 us: reduce_gradients(): wire = total.astype(BF)]
    pallas_call x0 -> x8, Pallas kernels: none -> 61.8 us  [the longest x1 34.4 us: mlp(): pl.pallas_call(mlp_kernel, out_shape=[share] * 8 + [jax.ShapeDtypeStruct(...]
    all_to_all x2 -> x0, blocking collectives: 49.3 us -> none  [the longest x1 25.2 us: body(): lax.all_to_all(conv_out, 'ch', split_axis=1, concat_axis=0, tiled=True)]
    ppermute x4 -> x33, waiting for transfers between devices: 0.01 us -> 44.2 us  [the longest x13 30.3 us: lon_swap(): return lax.ppermute(x, 'lon', [(i, i ^ k) for i in range(32)])]
    ppermute x4 -> x33, starting transfers between devices: 17.3 us -> 56.6 us  [the longest x15 25.4 us: ch_swap(): return lax.ppermute(x, 'ch', [(i, i ^ k) for i in range(4)])]
    all_to_all x2 -> x0, waiting for transfers between devices: 29 us -> none  [the longest x1 20 us: body(): lax.all_to_all(branch_cells.reshape(full_width, quarter, lon_cells), 'ch'...]
    dot_general x6 -> x12, matrix products: 51.3 us -> 23 us  [the longest x10 21.9 us: dotg(): lax.dot_general(a, b, (((ca,), (cb,)), ((), ())), preferred_element_type=...]
  transfers between devices with their start and end apart: 7 -> 33, of which waited for: 3 -> 10; matrix products, arithmetic and copies ran while one was open for 19% -> 20% of each run, Pallas kernels for 0% -> 11%
where the time goes in v1:
time: 243 us; the launch traced here: 242 us
  Pallas kernels  61.8 us (25%)
  starting transfers between devices  56.6 us (23%)
  local copies, waits for them, and re-layouts  48.2 us (20%)
  waiting for transfers between devices  44.2 us (18%)
  matrix products  23 us (9%)
  other arithmetic  7.51 us (3%)
    pallas_call x1, Pallas kernels, mlp(): pl.pallas_call(mlp_kernel, out_shape=[share] * 8 + [jax.ShapeDtypeStruct(...  34.4 us
    ppermute x13, waiting for transfers between devices, lon_swap(): return lax.ppermute(x, 'lon', [(i, i ^ k) for i in range(32)])  30.3 us
    ppermute x15, starting transfers between devices, ch_swap(): return lax.ppermute(x, 'ch', [(i, i ^ k) for i in range(4)])  25.4 us
    dot_general x10, matrix products, dotg(): lax.dot_general(a, b, (((ca,), (cb,)), ((), ())), preferred_element_type=...  21.9 us
    ppermute x13, starting transfers between devices, lon_swap(): return lax.ppermute(x, 'lon', [(i, i ^ k) for i in range(32)])  16.6 us
    ppermute x4, starting transfers between devices, lon_shift(): return lax.ppermute(x, 'lon', [(i, (i + d) % 32) for i in range(32)])  12.4 us
    ppermute x15, waiting for transfers between devices, ch_swap(): return lax.ppermute(x, 'ch', [(i, i ^ k) for i in range(4)])  11.3 us
    pallas_call x1, Pallas kernels, conv_backward(): pl.pallas_call(backward_kernel, out_shape=jax.ShapeDtypeStruct((LC, ROWS,...  10.2 us
  transfers between devices with their start and end apart: 33, of which 10 were waited for; matrix products, arithmetic and copies ran while one was open for 20% of the time, Pallas kernels for 11%

profile of v1, /device:TPU:1, one launch (start us, length us, event | category | flops | bytes accessed | tf_op | source)
XLA Modules:
  0.0 242.4 jit_solution(6889828086511912503)
XLA Ops:
  6.9 7.4 %collective-permute-start = (bf16[8,6400]{1,0:T(8,128)(2,1)}, bf16[8,6400]{1,0:T(8,128)(2,1)}, u32[]{:S(2)}, u32[]{:S(2)}) collective-permute-start(bf16[8,6400]{1,0:T(8,128)(2,1)} %convolution_convert_fusion.5), channel_id=1, source_target_pairs={{0,124},{4,0},{8,4},{12,8},{16,12},{20,16},{24,20},{28,24},{32,28}... | collective-permute-start | bytes 307208 | tf_op jit(solution)/shard_map/ppermute | solution.py:37
  22.9 8.9 %conv_forward.1 = (bf16[16,104,128]{2,1,0:T(8,128)(2,1)S(1)}, bf16[16,104,128]{2,1,0:T(8,128)(2,1)}, bf16[16,104,128]{2,1,0:T(8,128)(2,1)}, bf16[16,104,128]{2,1,0:T(8,128)(2,1)}) custom-call(s32[1]{0:T(128)} %bitcast.me_ref.refs_0_, bf16[100,64,128]{2,1,0:T(8,128)(2,1)S(1)} %copy-done.4, bf16[100,64,128]{2,1,0:T(8,128)(2,1)S(1)} %bitcast.66, ...), custom_call_target="tpu_custom_call" | custom-call | tf_op jit(solution)/shard_map/conv_forward/pallas_call | solution.py:114
  37.2 3.6 %copy.37.refs_10_ = bf16[1600,416]{1,0:T(8,128)(2,1)} copy(bf16[1600,416]{0,1:T(8,128)(2,1)} %bitcast.75) | data formatting | bytes 2662400 | tf_op jit(solution)/shard_map/convert_element_type | solution.py:416
  43.0 3.5 %copy.38.refs_12_ = bf16[1600,416]{1,0:T(8,128)(2,1)} copy(bf16[1600,416]{0,1:T(8,128)(2,1)} %bitcast.76) | data formatting | bytes 2662400 | tf_op jit(solution)/shard_map/convert_element_type | solution.py:417
  48.9 8.1 %collective-permute-done.4.refs_5_ = bf16[16,104,128]{2,1,0:T(8,128)(2,1)} collective-permute-done((bf16[16,104,128]{2,1,0:T(8,128)(2,1)}, bf16[16,104,128]{2,1,0:T(8,128)(2,1)}, u32[]{:S(2)}, u32[]{:S(2)}) %collective-permute-start.4) | collective-permute-done | bytes 426016 | tf_op jit(solution)/shard_map/ppermute | solution.py:33
  57.0 34.4 %mlp.1 = (bf16[16,104,128]{2,1,0:T(8,128)(2,1)}, bf16[16,104,128]{2,1,0:T(8,128)(2,1)}, bf16[16,104,128]{2,1,0:T(8,128)(2,1)}, bf16[16,104,128]{2,1,0:T(8,128)(2...) custom-call(s32[1]{0:T(128)} %bitcast.me_ref.refs_0_, ...), custom_call_target="tpu_custom_call" | custom-call | tf_op jit(solution)/shard_map/mlp/pallas_call | solution.py:253
  94.1 3.5 %copy.41 = bf16[1600,416]{0,1:T(8,128)(2,1)} copy(bf16[1600,416]{1,0:T(8,128)(2,1)} %slice_bitcast_fusion) | data formatting | bytes 2662400 | tf_op jit(solution)/shard_map/squeeze | solution.py:350
  97.9 3.2 %collective-permute-done.16 = bf16[1600,416]{0,1:T(8,128)(2,1)} collective-permute-done((bf16[1600,416]{0,1:T(8,128)(2,1)}, bf16[1600,416]{0,1:T(8,128)(2,1)}, u32[]{:S(2)}, u32[]{:S(2)}) %collective-permute-start.16) | collective-permute-done | bytes 1331232 | tf_op jit(solution)/shard_map/ppermute | solution.py:33
  101.1 3.5 %copy.42 = bf16[1600,416]{1,0:T(8,128)(2,1)} copy(bf16[1600,416]{0,1:T(8,128)(2,1)} %collective-permute-done.16) | data formatting | bytes 2662400 | tf_op jit(solution)/shard_map/ppermute | solution.py:33
  109.1 3.8 %collective-permute-start.19 = (bf16[400,416]{1,0:T(8,128)(2,1)S(1)}, bf16[400,416]{1,0:T(8,128)(2,1)}, u32[]{:S(2)}, u32[]{:S(2)}) collective-permute-start(bf16[400,416]{1,0:T(8,128)(2,1)S(1)} %get-tuple-element.41), channel_id=1, source_target_pairs={{0,12},{4,8},{8,4},{12,0},{16,28},{20,24},{24,20},{28,16},{32,44},... | collective-permute-start | bytes 998408 | tf_op jit(solution)/shard_map/ppermute | solution.py:41
  112.9 7.0 %collective-permute-done.17 = bf16[400,416]{1,0:T(8,128)(2,1)S(1)} collective-permute-done((bf16[400,416]{1,0:T(8,128)(2,1)S(1)}, bf16[400,416]{1,0:T(8,128)(2,1)S(1)}, u32[]{:S(2)}, u32[]{:S(2)}) %collective-permute-start.17) | collective-permute-done | bytes 332832 | tf_op jit(solution)/shard_map/ppermute | solution.py:41
  119.9 6.8 %collective-permute-done.18 = bf16[400,416]{1,0:T(8,128)(2,1)} collective-permute-done((bf16[400,416]{1,0:T(8,128)(2,1)S(1)}, bf16[400,416]{1,0:T(8,128)(2,1)}, u32[]{:S(2)}, u32[]{:S(2)}) %collective-permute-start.18) | collective-permute-done | bytes 332832 | tf_op jit(solution)/shard_map/ppermute | solution.py:41
  126.7 4.0 %collective-permute-done.19 = bf16[400,416]{1,0:T(8,128)(2,1)} collective-permute-done((bf16[400,416]{1,0:T(8,128)(2,1)S(1)}, bf16[400,416]{1,0:T(8,128)(2,1)}, u32[]{:S(2)}, u32[]{:S(2)}) %collective-permute-start.19) | collective-permute-done | bytes 332832 | tf_op jit(solution)/shard_map/ppermute | solution.py:41
  133.5 3.5 %collective-permute-start.22 = (bf16[104,416]{1,0:T(8,128)(2,1)S(1)}, bf16[104,416]{1,0:T(8,128)(2,1)S(1)}, u32[]{:S(2)}, u32[]{:S(2)}) collective-permute-start(bf16[104,416]{1,0:T(8,128)(2,1)S(1)} %get-tuple-element.48), channel_id=1, source_target_pairs={{0,48},{4,52},{8,56},{12,60},{16,32},{20,36},{24,40},{28,44},{32,1... | collective-permute-start | bytes 259592 | tf_op jit(solution)/shard_map/ppermute | solution.py:41
  149.0 3.3 %collective-permute-start.27 = (bf16[104,416]{1,0:T(8,128)(2,1)S(1)}, bf16[104,416]{1,0:T(8,128)(2,1)S(1)}, u32[]{:S(2)}, u32[]{:S(2)}) collective-permute-start(bf16[104,416]{1,0:T(8,128)(2,1)S(1)} %add_convert_fusion), channel_id=1, source_target_pairs={{0,32},{4,36},{8,40},{12,44},{16,48},{20,52},{24,56},{28,60},{32,0... | collective-permute-start | bytes 259592 | tf_op jit(solution)/shard_map/ppermute | solution.py:41
  152.8 5.1 %collective-permute-start.13 = (bf16[16,104,128]{2,1,0:T(8,128)(2,1)}, bf16[16,104,128]{2,1,0:T(8,128)(2,1)S(1)}, u32[]{:S(2)}, u32[]{:S(2)}) collective-permute-start(bf16[16,104,128]{2,1,0:T(8,128)(2,1)} %get-tuple-element.28), channel_id=1, source_target_pairs={{0,3},{1,2},{2,1},{3,0},{4,7},{5,6},{6,5},{7,4},{8,11},{9,10},{10,... | collective-permute-start | bytes 1277960 | tf_op jit(solution)/shard_map/ppermute | solution.py:33
  173.4 3.2 %collective-permute-start.30 = (bf16[400,416]{0,1:T(8,128)(2,1)}, bf16[400,416]{0,1:T(8,128)(2,1)}, u32[]{:S(2)}, u32[]{:S(2)}) collective-permute-start(bf16[400,416]{0,1:T(8,128)(2,1)} %dynamic_update_slice.15), channel_id=1, source_target_pairs={{0,8},{4,12},{8,0},{12,4},{16,24},{20,28},{24,16},{28,20},{32,40},... | collective-permute-start | bytes 998408 | tf_op jit(solution)/shard_map/ppermute | solution.py:41
  177.3 4.0 %collective-permute-start.10 = (bf16[16,104,128]{2,1,0:T(8,128)(2,1)}, bf16[16,104,128]{2,1,0:T(8,128)(2,1)}, u32[]{:S(2)}, u32[]{:S(2)}) collective-permute-start(bf16[16,104,128]{2,1,0:T(8,128)(2,1)} %get-tuple-element.24), channel_id=1, source_target_pairs={{0,3},{1,2},{2,1},{3,0},{4,7},{5,6},{6,5},{7,4},{8,11},{9,10},{10,... | collective-permute-start | bytes 1277960 | tf_op jit(solution)/shard_map/ppermute | solution.py:33
  184.2 7.8 %collective-permute-done.30 = bf16[400,416]{0,1:T(8,128)(2,1)} collective-permute-done((bf16[400,416]{0,1:T(8,128)(2,1)}, bf16[400,416]{0,1:T(8,128)(2,1)}, u32[]{:S(2)}, u32[]{:S(2)}) %collective-permute-start.30) | collective-permute-done | bytes 332832 | tf_op jit(solution)/shard_map/ppermute | solution.py:41
  194.9 4.0 %concatenate.25 = bf16[1600,416]{0,1:T(8,128)(2,1)} concatenate(bf16[400,416]{0,1:T(8,128)(2,1)} %get-tuple-element.35, bf16[400,416]{0,1:T(8,128)(2,1)} %get-tuple-element.34, bf16[400,416]{0,1:T(8,128)(2,1)} %get-tuple-element.33, bf16[400,416]{0,1:T(8,128)(2,1)} %get-tuple-element.32), dimensions={0} | concatenate | bytes 2662400 | tf_op jit(solution)/shard_map/concatenate | solution.py:382
  198.9 7.4 %collective-permute-start.32 = (bf16[1600,416]{0,1:T(8,128)(2,1)}, bf16[1600,416]{0,1:T(8,128)(2,1)}, u32[]{:S(2)}, u32[]{:S(2)}) collective-permute-start(bf16[1600,416]{0,1:T(8,128)(2,1)} %concatenate.25), channel_id=1, source_target_pairs={{0,1},{1,0},{2,3},{3,2},{4,5},{5,4},{6,7},{7,6},{8,9},{9,8},{10,11... | collective-permute-start | bytes 3993608 | tf_op jit(solution)/shard_map/ppermute | solution.py:33
  218.2 4.4 %update.1 = bf16[100,64,128]{2,1,0:T(8,128)(2,1)} custom-call(s32[1]{0:T(128)} %bitcast.me_ref.refs_0_, bf16[16,104,128]{2,1,0:T(8,128)(2,1)S(1)} %copy-done.10, bf16[16,104,128]{2,1,0:T(8,128)(2,1)} %collective-permute-done.8.b1, bf16[16,104,128]{2,1,0:T(8,128)(2,1)} %collective-permute-done.9.b2, bf16[16,104,128]{2,1,0:T(8,128)(2,1)} %collective-permute-done.10.b3, ...), custom_call_target="tpu_custom_call" | custom-call | tf_op jit(solution)/shard_map/update/pallas_call | solution.py:299
  225.8 10.2 %conv_backward.1 = bf16[100,64,128]{2,1,0:T(8,128)(2,1)} custom-call(s32[1]{0:T(128)} %bitcast.me_ref.refs_0_, bf16[16,104,128]{2,1,0:T(8,128)(2,1)S(1)} %copy-done.6, bf16[16,104,128]{2,1,0:T(8,128)(2,1)S(1)} %collective-permute-done.11.g1, bf16[16,104,128]{2,1,0:T(8,128)(2,1)S(1)} %collective-permute-done.12.g2, ...), custom_call_target="tpu_custom_call" | custom-call | tf_op jit(solution)/shard_map/conv_backward/pallas_call | solution.py:152
  238.5 3.8 %convolution_multiply_fusion.1 = f32[400,1600]{1,0:T(8,128)} fusion(bf16[1600,416]{0,1:T(8,128)(2,1)S(1)} %copy-done.14, bf16[1600,416]{0,1:T(8,128)(2,1)} %collective-permute-done.32, pred[]{:T(512)S(6)} %eq.149, s32[400]{0:T(512)S(1)} %fusion.31), kind=kOutput, calls=%fused_computation.8 | convolution fusion | flops 533952000 | bytes 5224001 | tf_op jit(solution)/shard_map/dot_general | solution.py:29
  (157 shorter events, 87.0 us)
Async XLA Ops:
  3.5 17.4 %collective-permute-start.1 = (bf16[8,6400]{1,0:T(8,128)(2,1)}, bf16[8,6400]{1,0:T(8,128)(2,1)}, u32[]{:S(2)}, u32[]{:S(2)}) collective-permute-start(bf16[8,6400]{1,0:T(8,128)(2,1)} %convolution_convert_fusion.4), channel_id=1, source_target_pairs={{0,4},{4,8},{8,12},{12,16},{16,20},{20,24},{24,28},{28,32},{32,36}... | collective-permute-start | bytes 307208 | tf_op jit(solution)/shard_map/ppermute | solution.py:37
  6.9 14.1 %collective-permute-start = (bf16[8,6400]{1,0:T(8,128)(2,1)}, bf16[8,6400]{1,0:T(8,128)(2,1)}, u32[]{:S(2)}, u32[]{:S(2)}) collective-permute-start(bf16[8,6400]{1,0:T(8,128)(2,1)} %convolution_convert_fusion.5), channel_id=1, source_target_pairs={{0,124},{4,0},{8,4},{12,8},{16,12},{20,16},{24,20},{28,24},{32,28}... | collective-permute-start | bytes 307208 | tf_op jit(solution)/shard_map/ppermute | solution.py:37
  15.6 16.7 %collective-permute-start.5 = (bf16[16,104,128]{2,1,0:T(8,128)(2,1)}, bf16[16,104,128]{2,1,0:T(8,128)(2,1)}, u32[]{:S(2)}, u32[]{:S(2)}) collective-permute-start(bf16[16,104,128]{2,1,0:T(8,128)(2,1)} %branch_share.5), channel_id=1, source_target_pairs={{0,1},{1,0},{2,3},{3,2},{4,5},{5,4},{6,7},{7,6},{8,9},{9,8},{10,11... | collective-permute-start | bytes 1277960 | tf_op jit(solution)/shard_map/ppermute | solution.py:33
  17.7 31.1 %collective-permute-start.6 = (bf16[16,104,128]{2,1,0:T(8,128)(2,1)}, bf16[16,104,128]{2,1,0:T(8,128)(2,1)}, u32[]{:S(2)}, u32[]{:S(2)}) collective-permute-start(bf16[16,104,128]{2,1,0:T(8,128)(2,1)} %branch_share.6), channel_id=1, source_target_pairs={{0,2},{1,3},{2,0},{3,1},{4,6},{5,7},{6,4},{7,5},{8,10},{9,11},{10,... | collective-permute-start | bytes 1277960 | tf_op jit(solution)/shard_map/ppermute | solution.py:33
  19.2 29.6 %collective-permute-start.7 = (bf16[16,104,128]{2,1,0:T(8,128)(2,1)}, bf16[16,104,128]{2,1,0:T(8,128)(2,1)}, u32[]{:S(2)}, u32[]{:S(2)}) collective-permute-start(bf16[16,104,128]{2,1,0:T(8,128)(2,1)} %branch_share.7), channel_id=1, source_target_pairs={{0,3},{1,2},{2,1},{3,0},{4,7},{5,6},{6,5},{7,4},{8,11},{9,10},{10,... | collective-permute-start | bytes 1277960 | tf_op jit(solution)/shard_map/ppermute | solution.py:33
  31.7 17.1 %collective-permute-start.2 = (bf16[16,104,128]{2,1,0:T(8,128)(2,1)}, bf16[16,104,128]{2,1,0:T(8,128)(2,1)S(1)}, u32[]{:S(2)}, u32[]{:S(2)}) collective-permute-start(bf16[16,104,128]{2,1,0:T(8,128)(2,1)} %get-tuple-element.18), channel_id=1, source_target_pairs={{0,1},{1,0},{2,3},{3,2},{4,5},{5,4},{6,7},{7,6},{8,9},{9,8},{10,11... | collective-permute-start | bytes 1277960 | tf_op jit(solution)/shard_map/ppermute | solution.py:33
  32.0 16.9 %collective-permute-start.3 = (bf16[16,104,128]{2,1,0:T(8,128)(2,1)}, bf16[16,104,128]{2,1,0:T(8,128)(2,1)}, u32[]{:S(2)}, u32[]{:S(2)}) collective-permute-start(bf16[16,104,128]{2,1,0:T(8,128)(2,1)} %get-tuple-element.19), channel_id=1, source_target_pairs={{0,2},{1,3},{2,0},{3,1},{4,6},{5,7},{6,4},{7,5},{8,10},{9,11},{10,... | collective-permute-start | bytes 1277960 | tf_op jit(solution)/shard_map/ppermute | solution.py:33
  32.3 24.7 %collective-permute-start.4 = (bf16[16,104,128]{2,1,0:T(8,128)(2,1)}, bf16[16,104,128]{2,1,0:T(8,128)(2,1)}, u32[]{:S(2)}, u32[]{:S(2)}) collective-permute-start(bf16[16,104,128]{2,1,0:T(8,128)(2,1)} %get-tuple-element.20), channel_id=1, source_target_pairs={{0,3},{1,2},{2,1},{3,0},{4,7},{5,6},{6,5},{7,4},{8,11},{9,10},{10,... | collective-permute-start | bytes 1277960 | tf_op jit(solution)/shard_map/ppermute | solution.py:33
  108.7 11.2 %collective-permute-start.17 = (bf16[400,416]{1,0:T(8,128)(2,1)S(1)}, bf16[400,416]{1,0:T(8,128)(2,1)S(1)}, u32[]{:S(2)}, u32[]{:S(2)}) collective-permute-start(bf16[400,416]{1,0:T(8,128)(2,1)S(1)} %get-tuple-element.40), channel_id=1, source_target_pairs={{0,4},{4,0},{8,12},{12,8},{16,20},{20,16},{24,28},{28,24},{32,36},... | collective-permute-start | bytes 998408 | tf_op jit(solution)/shard_map/ppermute | solution.py:41
  109.0 17.7 %collective-permute-start.18 = (bf16[400,416]{1,0:T(8,128)(2,1)S(1)}, bf16[400,416]{1,0:T(8,128)(2,1)}, u32[]{:S(2)}, u32[]{:S(2)}) collective-permute-start(bf16[400,416]{1,0:T(8,128)(2,1)S(1)} %get-tuple-element.42), channel_id=1, source_target_pairs={{0,8},{4,12},{8,0},{12,4},{16,24},{20,28},{24,16},{28,20},{32,40},... | collective-permute-start | bytes 998408 | tf_op jit(solution)/shard_map/ppermute | solution.py:41
  109.1 21.6 %collective-permute-start.19 = (bf16[400,416]{1,0:T(8,128)(2,1)S(1)}, bf16[400,416]{1,0:T(8,128)(2,1)}, u32[]{:S(2)}, u32[]{:S(2)}) collective-permute-start(bf16[400,416]{1,0:T(8,128)(2,1)S(1)} %get-tuple-element.41), channel_id=1, source_target_pairs={{0,12},{4,8},{8,4},{12,0},{16,28},{20,24},{24,20},{28,16},{32,44},... | collective-permute-start | bytes 998408 | tf_op jit(solution)/shard_map/ppermute | solution.py:41
  145.0 31.7 %collective-permute-start.11 = (bf16[16,104,128]{2,1,0:T(8,128)(2,1)}, bf16[16,104,128]{2,1,0:T(8,128)(2,1)S(1)}, u32[]{:S(2)}, u32[]{:S(2)}) collective-permute-start(bf16[16,104,128]{2,1,0:T(8,128)(2,1)} %get-tuple-element.26), channel_id=1, source_target_pairs={{0,1},{1,0},{2,3},{3,2},{4,5},{5,4},{6,7},{7,6},{8,9},{9,8},{10,11... | collective-permute-start | bytes 1277960 | tf_op jit(solution)/shard_map/ppermute | solution.py:33
  149.0 8.9 %collective-permute-start.27 = (bf16[104,416]{1,0:T(8,128)(2,1)S(1)}, bf16[104,416]{1,0:T(8,128)(2,1)S(1)}, u32[]{:S(2)}, u32[]{:S(2)}) collective-permute-start(bf16[104,416]{1,0:T(8,128)(2,1)S(1)} %add_convert_fusion), channel_id=1, source_target_pairs={{0,32},{4,36},{8,40},{12,44},{16,48},{20,52},{24,56},{28,60},{32,0... | collective-permute-start | bytes 259592 | tf_op jit(solution)/shard_map/ppermute | solution.py:41
  152.8 24.5 %collective-permute-start.12 = (bf16[16,104,128]{2,1,0:T(8,128)(2,1)}, bf16[16,104,128]{2,1,0:T(8,128)(2,1)S(1)}, u32[]{:S(2)}, u32[]{:S(2)}) collective-permute-start(bf16[16,104,128]{2,1,0:T(8,128)(2,1)} %get-tuple-element.27), channel_id=1, source_target_pairs={{0,2},{1,3},{2,0},{3,1},{4,6},{5,7},{6,4},{7,5},{8,10},{9,11},{10,... | collective-permute-start | bytes 1277960 | tf_op jit(solution)/shard_map/ppermute | solution.py:33
  152.8 28.5 %collective-permute-start.13 = (bf16[16,104,128]{2,1,0:T(8,128)(2,1)}, bf16[16,104,128]{2,1,0:T(8,128)(2,1)S(1)}, u32[]{:S(2)}, u32[]{:S(2)}) collective-permute-start(bf16[16,104,128]{2,1,0:T(8,128)(2,1)} %get-tuple-element.28), channel_id=1, source_target_pairs={{0,3},{1,2},{2,1},{3,0},{4,7},{5,6},{6,5},{7,4},{8,11},{9,10},{10,... | collective-permute-start | bytes 1277960 | tf_op jit(solution)/shard_map/ppermute | solution.py:33
  173.4 9.6 %collective-permute-start.29 = (bf16[400,416]{0,1:T(8,128)(2,1)}, bf16[400,416]{0,1:T(8,128)(2,1)}, u32[]{:S(2)}, u32[]{:S(2)}) collective-permute-start(bf16[400,416]{0,1:T(8,128)(2,1)} %dynamic_update_slice.15), channel_id=1, source_target_pairs={{0,4},{4,0},{8,12},{12,8},{16,20},{20,16},{24,28},{28,24},{32,36},... | collective-permute-start | bytes 998408 | tf_op jit(solution)/shard_map/ppermute | solution.py:41
  173.4 18.7 %collective-permute-start.30 = (bf16[400,416]{0,1:T(8,128)(2,1)}, bf16[400,416]{0,1:T(8,128)(2,1)}, u32[]{:S(2)}, u32[]{:S(2)}) collective-permute-start(bf16[400,416]{0,1:T(8,128)(2,1)} %dynamic_update_slice.15), channel_id=1, source_target_pairs={{0,8},{4,12},{8,0},{12,4},{16,24},{20,28},{24,16},{28,20},{32,40},... | collective-permute-start | bytes 998408 | tf_op jit(solution)/shard_map/ppermute | solution.py:41
  176.7 15.4 %collective-permute-start.31 = (bf16[400,416]{0,1:T(8,128)(2,1)}, bf16[400,416]{0,1:T(8,128)(2,1)}, u32[]{:S(2)}, u32[]{:S(2)}) collective-permute-start(bf16[400,416]{0,1:T(8,128)(2,1)} %dynamic_update_slice.15), channel_id=1, source_target_pairs={{0,12},{4,8},{8,4},{12,0},{16,28},{20,24},{24,20},{28,16},{32,44},... | collective-permute-start | bytes 998408 | tf_op jit(solution)/shard_map/ppermute | solution.py:41
  177.3 35.8 %collective-permute-start.10 = (bf16[16,104,128]{2,1,0:T(8,128)(2,1)}, bf16[16,104,128]{2,1,0:T(8,128)(2,1)}, u32[]{:S(2)}, u32[]{:S(2)}) collective-permute-start(bf16[16,104,128]{2,1,0:T(8,128)(2,1)} %get-tuple-element.24), channel_id=1, source_target_pairs={{0,3},{1,2},{2,1},{3,0},{4,7},{5,6},{6,5},{7,4},{8,11},{9,10},{10,... | collective-permute-start | bytes 1277960 | tf_op jit(solution)/shard_map/ppermute | solution.py:33
  181.3 34.4 %collective-permute-start.8 = (bf16[16,104,128]{2,1,0:T(8,128)(2,1)}, bf16[16,104,128]{2,1,0:T(8,128)(2,1)}, u32[]{:S(2)}, u32[]{:S(2)}) collective-permute-start(bf16[16,104,128]{2,1,0:T(8,128)(2,1)} %get-tuple-element.22), channel_id=1, source_target_pairs={{0,1},{1,0},{2,3},{3,2},{4,5},{5,4},{6,7},{7,6},{8,9},{9,8},{10,11... | collective-permute-start | bytes 1277960 | tf_op jit(solution)/shard_map/ppermute | solution.py:33
  183.0 32.8 %collective-permute-start.9 = (bf16[16,104,128]{2,1,0:T(8,128)(2,1)}, bf16[16,104,128]{2,1,0:T(8,128)(2,1)}, u32[]{:S(2)}, u32[]{:S(2)}) collective-permute-start(bf16[16,104,128]{2,1,0:T(8,128)(2,1)} %get-tuple-element.23), channel_id=1, source_target_pairs={{0,2},{1,3},{2,0},{3,1},{4,6},{5,7},{6,4},{7,5},{8,10},{9,11},{10,... | collective-permute-start | bytes 1277960 | tf_op jit(solution)/shard_map/ppermute | solution.py:33
  198.9 37.1 %collective-permute-start.32 = (bf16[1600,416]{0,1:T(8,128)(2,1)}, bf16[1600,416]{0,1:T(8,128)(2,1)}, u32[]{:S(2)}, u32[]{:S(2)}) collective-permute-start(bf16[1600,416]{0,1:T(8,128)(2,1)} %concatenate.25), channel_id=1, source_target_pairs={{0,1},{1,0},{2,3},{3,2},{4,5},{5,4},{6,7},{7,6},{8,9},{9,8},{10,11... | collective-permute-start | bytes 3993608 | tf_op jit(solution)/shard_map/ppermute | solution.py:33
  209.0 13.5 %collective-permute-start.14 = (bf16[8,6656]{1,0:T(8,128)(2,1)}, bf16[8,6656]{1,0:T(8,128)(2,1)}, u32[]{:S(2)}, u32[]{:S(2)}) collective-permute-start(bf16[8,6656]{1,0:T(8,128)(2,1)} %convolution_convert_fusion.3), channel_id=1, source_target_pairs={{0,124},{4,0},{8,4},{12,8},{16,12},{20,16},{24,20},{28,24},{32,28}... | collective-permute-start | bytes 319496 | tf_op jit(solution)/shard_map/ppermute | solution.py:37
  213.1 10.2 %collective-permute-start.15 = (bf16[8,6656]{1,0:T(8,128)(2,1)}, bf16[8,6656]{1,0:T(8,128)(2,1)}, u32[]{:S(2)}, u32[]{:S(2)}) collective-permute-start(bf16[8,6656]{1,0:T(8,128)(2,1)} %convolution_convert_fusion.2), channel_id=1, source_target_pairs={{0,4},{4,8},{8,12},{12,16},{16,20},{20,24},{24,28},{28,32},{32,36}... | collective-permute-start | bytes 319496 | tf_op jit(solution)/shard_map/ppermute | solution.py:37
  (34 other events, 240.5 us)

commit v2 on v1

--- a/solution.py
+++ b/solution.py
@@ -27,6 +27,10 @@
 
 def dotg(a, b, ca, cb):
     return lax.dot_general(a, b, (((ca,), (cb,)), ((), ())), preferred_element_type=F32)
+
+
+def cost(micros):
+    return pl.CostEstimate(flops=0, bytes_accessed=int(micros * 3.3e6), transcendentals=0)
 
 
 def ch_swap(x, k):
@@ -64,6 +68,7 @@
             out_specs=pl.BlockSpec((QR, CP, LANES), lambda i, me: (0, 0, 0)),
         ),
         compiler_params=pltpu.CompilerParams(vmem_limit_bytes=32 << 20),
+        cost_estimate=cost(1.2),
         name="branch_share",
     )(me, cotangent, sea_mask, scale)
 
@@ -127,6 +132,7 @@
             scratch_shapes=[pltpu.VMEM((4, QR, GROUP, LANES), F32)],
         ),
         compiler_params=pltpu.CompilerParams(vmem_limit_bytes=32 << 20),
+        cost_estimate=cost(9),
         name="conv_forward",
     )(me, state, rim, pattern, bias)
 
@@ -165,13 +171,16 @@
             scratch_shapes=[pltpu.VMEM((4, QR, GROUP, LANES), F32)] * 2,
         ),
         compiler_params=pltpu.CompilerParams(vmem_limit_bytes=32 << 20),
+        cost_estimate=cost(10),
         name="conv_backward",
     )(me, *grads, *rims, pattern, cotangent, sea_mask)
 
 
-CHUNK = 4
+CHUNK = 8
 CELLS = CHUNK * LANES
 HT = 400
+PIECE = 328
+WIRE = 16 * PIECE
 
 
 def mlp_kernel(*refs):
@@ -179,8 +188,8 @@
     xs, gs = refs[2:6], refs[6:10]
     win_t, win, wout, wout_t, vec, bias_in = refs[10:16]
     brs, gcs = refs[16:20], refs[20:24]
-    wgrad = refs[24]
-    x_all, g_all, act, gpre, sum_in, sum_out = refs[25:]
+    keep, send = refs[24:26]
+    x_all, g_all, act, gpre, sums = refs[26:]
     step = pl.program_id(0)
     me = me_ref[0]
     for k in range(4):
@@ -226,19 +235,25 @@
 
     @pl.when(step == 0)
     def _():
-        sum_in[...] = part_in
-        sum_out[...] = part_out
+        sums[0] = part_in
+        sums[1] = part_out
 
     @pl.when(step > 0)
     def _():
-        sum_in[...] += part_in
-        sum_out[...] += part_out
+        sums[0] += part_in
+        sums[1] += part_out
 
     @pl.when(step == pl.num_programs(0) - 1)
     def _():
         core = core_ref[0]
-        wgrad[core] = sum_in[...].astype(BF)
-        wgrad[1 - core] = sum_out[...].astype(BF)
+        for out, slot in ((keep, core), (send, 1 - core)):
+            for t in range(3):
+                out[t * HID : (t + 1) * HID, :] = sums[slot, :, t * LANES : (t + 1) * LANES].astype(BF)
+            rest = [
+                sums[slot, q * 400 : (q + 1) * 400, 3 * LANES : 4 * CP] for q in range(4)
+            ]
+            out[3 * HID : 3 * HID + 400, :] = jnp.concatenate(rest, axis=1).astype(BF)
+            out[3 * HID + 400 :, :] = jnp.zeros((WIRE - 3 * HID - 400, LANES), BF)
 
 
 def mlp(me, core, xs, gs, weights, vec, bias_in):
@@ -252,7 +267,7 @@
     share = jax.ShapeDtypeStruct((QR, CP, LANES), BF)
     outs = pl.pallas_call(
         mlp_kernel,
-        out_shape=[share] * 8 + [jax.ShapeDtypeStruct((2, HID, 4 * CP), BF)],
+        out_shape=[share] * 8 + [jax.ShapeDtypeStruct((WIRE, LANES), BF)] * 2,
         grid_spec=pltpu.PrefetchScalarGridSpec(
             num_scalar_prefetch=2,
             grid=(QR // CHUNK,),
@@ -265,20 +280,20 @@
                 whole((4 * CP, 3)),
                 whole((HID, 1)),
             ],
-            out_specs=[piece] * 8 + [whole((2, HID, 4 * CP))],
+            out_specs=[piece] * 8 + [whole((WIRE, LANES))] * 2,
             scratch_shapes=[
                 pltpu.VMEM((4, CP, CELLS), F32),
                 pltpu.VMEM((4, CP, CELLS), F32),
                 pltpu.VMEM((HID, CELLS), BF),
                 pltpu.VMEM((HID, CELLS), BF),
-                pltpu.VMEM((HID, 4 * CP), F32),
-                pltpu.VMEM((HID, 4 * CP), F32),
+                pltpu.VMEM((2, HID, 4 * CP), F32),
             ],
         ),
         compiler_params=pltpu.CompilerParams(vmem_limit_bytes=56 << 20),
+        cost_estimate=cost(34),
         name="mlp",
     )(me, core, *xs, *gs, *weights, vec, bias_in)
-    return outs[:4], outs[4:8], outs[8]
+    return outs[:4], outs[4:8], outs[8], outs[9]
 
 
 def update_kernel(me_ref, b0, b1, b2, b3, state_ref, mask_ref, scale_ref, out_ref):
@@ -311,8 +326,31 @@
             out_specs=pl.BlockSpec((LC, QR, LANES), lambda i, me: (0, me[0] ^ i, 0)),
         ),
         compiler_params=pltpu.CompilerParams(vmem_limit_bytes=32 << 20),
+        cost_estimate=cost(4.4),
         name="update",
     )(me, *pieces, state, sea_mask, scale)
+
+
+def weights_kernel(one, two, pad, one_out, one_t, two_out, two_t):
+    for source, out, turned in ((one, one_out, one_t), (two, two_out, two_t)):
+        padded = dotg(pad[...], source[...], 0, 0)
+        out[...] = padded.astype(BF)
+        turned[...] = padded.T.astype(BF)
+
+
+def padded_weights(one, two, pad):
+    vmem = pl.BlockSpec(memory_space=pltpu.VMEM)
+    flat = jax.ShapeDtypeStruct((4 * CP, HID), BF)
+    turned = jax.ShapeDtypeStruct((HID, 4 * CP), BF)
+    return pl.pallas_call(
+        weights_kernel,
+        out_shape=[flat, turned, flat, turned],
+        in_specs=[vmem] * 3,
+        out_specs=[vmem] * 4,
+        compiler_params=pltpu.CompilerParams(vmem_limit_bytes=48 << 20),
+        cost_estimate=cost(5),
+        name="padded_weights",
+    )(one, two, pad)
 
 
 def tap_patterns(kernel):
@@ -334,53 +372,117 @@
     return head, tail
 
 
-def rims(cells2d):
-    head, tail = edge_picks()
-    first = dotg(head, cells2d, 1, 1).astype(BF)
-    last = dotg(tail, cells2d, 1, 1).astype(BF)
+def edges_kernel(cells, pick, *refs):
+    both = dotg(pick[...], cells[...], 1, 1)
+    refs[-2][...] = both[:8].astype(BF)
+    refs[-1][...] = both[8:].astype(BF)
+
+
+def edges(cells2d, picks, after=()):
+    vmem = pl.BlockSpec(memory_space=pltpu.VMEM)
+    out = jax.ShapeDtypeStruct((8, cells2d.shape[0]), BF)
+    return pl.pallas_call(
+        edges_kernel,
+        out_shape=[out, out],
+        in_specs=[vmem, vmem] + [pl.BlockSpec(memory_space=pl.ANY)] * len(after),
+        out_specs=[vmem, vmem],
+        compiler_params=pltpu.CompilerParams(vmem_limit_bytes=32 << 20),
+        cost_estimate=cost(1.5),
+        name="edges",
+    )(cells2d, picks, *after)
+
+
+def rims(cells2d, after=()):
+    picks = jnp.concatenate(edge_picks(), 0)
+    first, last = edges(cells2d, picks, after)
     from_right = lon_shift(first, -1)
     from_left = lon_shift(last, 1)
-    return dotg(
-        jnp.concatenate([from_right, from_left], 0), jnp.concatenate([head, tail], 0), 0, 0
-    ).astype(BF)
-
-
-def reduce_gradients(wgrad, lon):
-    y, z = lon & 3, (lon >> 2) & 3
-    mine = wgrad[0].astype(F32) + ch_swap(wgrad[1], 1).astype(F32)
-    mine = mine.reshape(4, HID // 4, 4 * CP)
-    wire = mine.astype(BF)
-    total = lax.dynamic_index_in_dim(mine, y, 0, False)
-    for k in (1, 2, 3):
-        total = total + lon_swap(
-            lax.dynamic_index_in_dim(wire, y ^ k, 0, False), k
-        ).astype(F32)
-
-    def strip(a, i):
-        return lax.dynamic_slice_in_dim(a, jnp.minimum(i * 104, 296), 104, 0)
-
-    wire = total.astype(BF)
-    part = strip(total, z)
-    for k in (1, 2, 3):
-        part = part + lon_swap(strip(wire, z ^ k), 4 * k).astype(F32)
-    wire = part.astype(BF)
+    both = [from_right, from_left]
+    return dotg(jnp.concatenate(both, 0), picks, 0, 0).astype(BF), both
+
+
+PLANES = [[16 * half + i for i in range(16)] for half in range(2)]
+
+
+def plane_exchange(pieces):
+    return lax.all_to_all(pieces, "lon", 0, 0, axis_index_groups=PLANES)
+
+
+def total_kernel(*refs):
+    total = refs[0][0].astype(F32)
+    for i in range(1, 16):
+        total = total + refs[0][i].astype(F32)
+    refs[-1][...] = total.astype(BF)
+
+
+def plane_total(pieces, after):
+    vmem = pl.BlockSpec(memory_space=pltpu.VMEM)
+    return pl.pallas_call(
+        total_kernel,
+        out_shape=jax.ShapeDtypeStruct((PIECE, LANES), BF),
+        in_specs=[vmem] + [pl.BlockSpec(memory_space=pl.ANY)] * len(after),
+        out_specs=vmem,
+        cost_estimate=cost(1.2),
+        name="plane_total",
+    )(pieces, *after)
+
+
+def copies_kernel(*refs):
+    for i in range(16):
+        refs[-1][i] = refs[0][...]
+
+
+def plane_copies(part, after):
+    vmem = pl.BlockSpec(memory_space=pltpu.VMEM)
+    return pl.pallas_call(
+        copies_kernel,
+        out_shape=jax.ShapeDtypeStruct((16, PIECE, LANES), BF),
+        in_specs=[vmem] + [pl.BlockSpec(memory_space=pl.ANY)] * len(after),
+        out_specs=vmem,
+        cost_estimate=cost(1),
+        name="plane_copies",
+    )(part, *after)
+
+
+def reduce_gradients(keep, send, early, late):
+    mine = keep.astype(F32) + ch_swap(send, 1).astype(F32)
+    mine = plane_exchange(mine.astype(BF).reshape(16, PIECE, LANES))
+    wire = plane_total(mine, early)
     part = (
         (wire.astype(F32) + lon_swap(wire, 16).astype(F32))
         + (ch_swap(wire, 2).astype(F32) + both_swap(wire).astype(F32))
     ).astype(BF)
-    others = [part] + [lon_swap(part, 4 * k) for k in (1, 2, 3)]
-    strips = jnp.stack(others)
-    block = jnp.zeros((HID // 4, 4 * CP), BF)
-    for k in range(4):
-        block = lax.dynamic_update_slice_in_dim(
-            block,
-            lax.dynamic_index_in_dim(strips, z ^ k, 0, False),
-            min(k * 104, 296),
-            0,
-        )
-    blocks = jnp.stack([block] + [lon_swap(block, k) for k in (1, 2, 3)])
-    full = jnp.concatenate([lax.dynamic_index_in_dim(blocks, y ^ k, 0, False) for k in range(4)], 0)
-    return full, ch_swap(full, 1)
+    return plane_exchange(plane_copies(part, late)).reshape(WIRE, LANES)
+
+
+def finish_kernel(core_ref, own, other, pad, grad_in, grad_out, held):
+    core = core_ref[0]
+    for wire, slot in ((own, core), (other, 1 - core)):
+        for t in range(3):
+            held[slot, :, t * LANES : (t + 1) * LANES] = wire[t * HID : (t + 1) * HID, :]
+        rest = wire[3 * HID : 3 * HID + 400, :]
+        for q in range(4):
+            held[slot, q * 400 : (q + 1) * 400, 3 * LANES :] = rest[:, q * 32 : (q + 1) * 32]
+    factor = 1.0 / math.sqrt(ROWS * LANES * 32)
+    grad_in[...] = dotg(pad[...], held[0], 1, 1) * factor
+    grad_out[...] = dotg(pad[...], held[1], 1, 1) * factor
+
+
+def finish(core, own, other, pad):
+    vmem = pl.BlockSpec(memory_space=pltpu.VMEM)
+    return pl.pallas_call(
+        finish_kernel,
+        out_shape=[
+            jax.ShapeDtypeStruct((C, HID), F32),
+            jax.ShapeDtypeStruct((C, HID), F32),
+        ],
+        in_specs=[pl.BlockSpec(memory_space=pltpu.SMEM)] + [vmem] * 3,
+        out_specs=[vmem] * 2,
+        scratch_shapes=[pltpu.VMEM((2, HID, 4 * CP), BF)],
+        compiler_params=pltpu.CompilerParams(vmem_limit_bytes=32 << 20),
+        cost_estimate=cost(6),
+        name="finish",
+    )(core, own, other, pad)
 
 
 def both_swap(x):
@@ -402,7 +504,6 @@
     cotangent,
 ):
     ch = lax.axis_index("ch")
-    lon = lax.axis_index("lon")
     me = ch.reshape(1)
     core = (ch & 1).reshape(1)
     scale = jnp.pad(layer_scale, (0, CP - LC)).reshape(CP, 1)
@@ -412,19 +513,17 @@
 
     chan = jnp.arange(C)
     pad = ((chan // LC * CP + chan % LC)[:, None] == jnp.arange(4 * CP)[None, :]).astype(BF)
-    win = dotg(pad, weight_in, 0, 0).astype(BF)
-    win_t = dotg(weight_in, pad, 0, 0).astype(BF)
-    wout = dotg(weight_out, pad, 1, 0).astype(BF)
-    wout_t = dotg(pad, weight_out, 0, 1).astype(BF)
+    win, win_t, wout_t, wout = padded_weights(weight_in, weight_out.T, pad)
     vec = jnp.stack([norm_gain, norm_bias, bias_out], 1).reshape(4, LC, 3)
     vec = jnp.pad(vec, ((0, 0), (0, CP - LC), (0, 0))).reshape(4 * CP, 3)
 
-    state_rim = rims(ocean_state.reshape(LC * ROWS, LANES)).reshape(LC, ROWS, LANES)
+    state_rim, _ = rims(ocean_state.reshape(LC * ROWS, LANES), (sent[2], sent[3]))
+    state_rim = state_rim.reshape(LC, ROWS, LANES)
     bias = jnp.broadcast_to(conv_bias[:, None, None], (LC, 1, LANES))
     conv = conv_forward(me, ocean_state, state_rim, tap_patterns(kernel), bias)
     xs = [conv[0]] + [ch_swap(conv[k], k) for k in (1, 2, 3)]
 
-    branch, grad, wgrad = mlp(
+    branch, grad, keep, send = mlp(
         me, core, xs, gs, (win_t, win, wout, wout_t), vec, bias_in.reshape(HID, 1)
     )
 
@@ -432,7 +531,10 @@
     pieces = [branch[0]] + [ch_swap(branch[k], k) for k in (1, 2, 3)]
 
     every = jnp.concatenate(grads, 0).reshape(4 * QR * CP, LANES)
-    grad_rims = rims(every).reshape(4, QR, CP, LANES)
+    grad_rims, arrived = rims(every)
+    grad_rims = grad_rims.reshape(4, QR, CP, LANES)
+    own = reduce_gradients(keep, send, arrived, pieces)
+
     grad_state = conv_backward(
         me,
         grads,
@@ -443,17 +545,9 @@
     )
     updated = update(me, pieces, ocean_state, sea_mask, scale)
 
-    full, other = reduce_gradients(wgrad, lon)
-    first = (ch & 1) == 0
-    grad_in = jnp.where(first, full, other)
-    grad_out = jnp.where(first, other, full)
-    grad_scale = 1.0 / math.sqrt(ROWS * LANES * lax.axis_size("lon"))
-    return (
-        updated,
-        grad_state,
-        dotg(pad, grad_in, 1, 1) * grad_scale,
-        dotg(grad_out, pad, 1, 1) * grad_scale,
-    )
+    own, grad_state, updated = lax.optimization_barrier((own, grad_state, updated))
+    grad_in, grad_out = finish(core, own, ch_swap(own, 1), pad)
+    return updated, grad_state, grad_in, grad_out.T
 
 
 def solution(mesh):

time: 243 us -> 216 us (0.89)
  local copies, waits for them, and re-layouts: 48.2 us -> 20 us
  waiting for transfers between devices: 44.2 us -> 67 us
  matrix products: 23 us -> 4.93 us
  starting transfers between devices: 56.6 us -> 39.9 us
  Pallas kernels: 61.8 us -> 76 us
    ppermute x15, waiting for transfers between devices: 11.3 us -> 32.9 us  [ch_swap(): return lax.ppermute(x, 'ch', [(i, i ^ k) for i in range(4)])]
    ppermute x13 -> x1, waiting for transfers between devices: 30.3 us -> 10.8 us  [lon_swap(): return lax.ppermute(x, 'lon', [(i, i ^ k) for i in range(32)])]
    dot_general x10 -> x2, matrix products: 21.9 us -> 3.13 us  [dotg(): lax.dot_general(a, b, (((ca,), (cb,)), ((), ())), preferred_element_type=...]
    ppermute x4, waiting for transfers between devices: 0.74 us -> 18.6 us  [lon_shift(): return lax.ppermute(x, 'lon', [(i, (i + d) % 32) for i in range(32)])]
    pallas_call x0 -> x6, Pallas kernels: none -> 15.3 us  [the longest x1 5.79 us: finish(): pl.pallas_call(finish_kernel, out_shape=[jax.ShapeDtypeStruct((C, HID), F...]
    ppermute x13 -> x1, starting transfers between devices: 16.6 us -> 2.45 us  [lon_swap(): return lax.ppermute(x, 'lon', [(i, i ^ k) for i in range(32)])]
    ppermute x15, starting transfers between devices: 25.4 us -> 13.5 us  [ch_swap(): return lax.ppermute(x, 'ch', [(i, i ^ k) for i in range(4)])]
    all_to_all x0 -> x2, starting transfers between devices: none -> 10.7 us  [plane_exchange(): return lax.all_to_all(pieces, 'lon', 0, 0, axis_index_groups=PLANES)]
  transfers between devices with their start and end apart: 33 -> 23, of which waited for: 10 -> 11; matrix products, arithmetic and copies ran while one was open for 20% -> 7% of each run, Pallas kernels for 11% -> 16%
where the time goes in v2:
time: 216 us; the launch traced here: 215 us
  Pallas kernels  76 us (35%)
  waiting for transfers between devices  67 us (31%)
  starting transfers between devices  39.9 us (18%)
  local copies, waits for them, and re-layouts  20 us (9%)
  other arithmetic  6.12 us (3%)
  matrix products  4.93 us (2%)
    pallas_call x1, Pallas kernels, mlp(): pl.pallas_call(mlp_kernel, out_shape=[share] * 8 + [jax.ShapeDtypeStruct(...  33.4 us
    ppermute x15, waiting for transfers between devices, ch_swap(): return lax.ppermute(x, 'ch', [(i, i ^ k) for i in range(4)])  32.9 us
    ppermute x4, waiting for transfers between devices, lon_shift(): return lax.ppermute(x, 'lon', [(i, (i + d) % 32) for i in range(32)])  18.6 us
    ppermute x15, starting transfers between devices, ch_swap(): return lax.ppermute(x, 'ch', [(i, i ^ k) for i in range(4)])  13.5 us
    ppermute x4, starting transfers between devices, lon_shift(): return lax.ppermute(x, 'lon', [(i, (i + d) % 32) for i in range(32)])  13.2 us
    unnamed x63, local copies, waits for them, and re-layouts  12.5 us
    ppermute x1, waiting for transfers between devices, lon_swap(): return lax.ppermute(x, 'lon', [(i, i ^ k) for i in range(32)])  10.8 us
    all_to_all x2, starting transfers between devices, plane_exchange(): return lax.all_to_all(pieces, 'lon', 0, 0, axis_index_groups=PLANES)  10.7 us
  transfers between devices with their start and end apart: 23, of which 11 were waited for; matrix products, arithmetic and copies ran while one was open for 7% of the time, Pallas kernels for 16%

profile of v2, /device:TPU:1, one launch (start us, length us, event | category | flops | bytes accessed | tf_op | source)
XLA Modules:
  0.0 214.7 jit_solution(11537989978178421419)
XLA Ops:
  10.3 8.8 %collective-permute-start = (bf16[8,6400]{1,0:T(8,128)(2,1)}, bf16[8,6400]{1,0:T(8,128)(2,1)}, u32[]{:S(2)}, u32[]{:S(2)}) collective-permute-start(bf16[8,6400]{1,0:T(8,128)(2,1)} %get-tuple-element.31), channel_id=1, source_target_pairs={{0,124},{4,0},{8,4},{12,8},{16,12},{20,16},{24,20},{28,24},{32,28}... | collective-permute-start | bytes 307208 | tf_op jit(solution)/shard_map/ppermute | solution.py:41
  26.9 8.8 %collective-permute-done.1 = bf16[8,6400]{1,0:T(8,128)(2,1)} collective-permute-done((bf16[8,6400]{1,0:T(8,128)(2,1)S(1)}, bf16[8,6400]{1,0:T(8,128)(2,1)}, u32[]{:S(2)}, u32[]{:S(2)}) %collective-permute-start.1) | collective-permute-done | bytes 102432 | tf_op jit(solution)/shard_map/ppermute | solution.py:41
  37.5 8.8 %conv_forward.1 = (bf16[16,104,128]{2,1,0:T(8,128)(2,1)S(1)}, bf16[16,104,128]{2,1,0:T(8,128)(2,1)}, bf16[16,104,128]{2,1,0:T(8,128)(2,1)}, bf16[16,104,128]{2,1,0:T(8,128)(2,1)}) custom-call(s32[1]{0:T(128)} %bitcast.me_ref.refs_0_, bf16[100,64,128]{2,1,0:T(8,128)(2,1)S(1)} %copy-done.2, bf16[100,64,128]{2,1,0:T(8,128)(2,1)S(1)} %bitcast.23, ...), custom_call_target="tpu_custom_call" | custom-call | bytes 29700000 | tf_op jit(solution)/shard_map/conv_forward/pallas_call | solution.py:119
  55.9 3.5 %padded_weights.1 = (bf16[416,1600]{1,0:T(8,128)(2,1)S(1)}, bf16[1600,416]{1,0:T(8,128)(2,1)}, bf16[416,1600]{1,0:T(8,128)(2,1)S(1)}, bf16[1600,416]{1,0:T(8,128)(2,1)}) custom-call(bf16[400,1600]{1,0:T(8,128)(2,1)S(1)} %copy-done.16, bf16[400,1600]{1,0:T(8,128)(2,1)S(1)} %bitcast.28, bf16[400,416]{1,0:T(8,128)(2,1)S(1)} %fusion.pad), custom_call_target="tpu_custom_call" | custom-call | bytes 16500000 | tf_op jit(solution)/shard_map/padded_weights/pallas_call | solution.py:345
  62.3 7.6 %collective-permute-done.4.refs_5_ = bf16[16,104,128]{2,1,0:T(8,128)(2,1)} collective-permute-done((bf16[16,104,128]{2,1,0:T(8,128)(2,1)}, bf16[16,104,128]{2,1,0:T(8,128)(2,1)}, u32[]{:S(2)}, u32[]{:S(2)}) %collective-permute-start.4) | collective-permute-done | bytes 426016 | tf_op jit(solution)/shard_map/ppermute | solution.py:37
  69.9 33.4 %mlp.1 = (bf16[16,104,128]{2,1,0:T(8,128)(2,1)}, bf16[16,104,128]{2,1,0:T(8,128)(2,1)}, bf16[16,104,128]{2,1,0:T(8,128)(2,1)}, bf16[16,104,128]{2,1,0:T(8,128)(2...) custom-call(s32[1]{0:T(128)} %bitcast.me_ref.refs_0_, ...), custom_call_target="tpu_custom_call" | custom-call | bytes 112200000 | tf_op jit(solution)/shard_map/mlp/pallas_call | solution.py:268
  103.8 3.0 %collective-permute-done.8 = bf16[5248,128]{1,0:T(8,128)(2,1)S(1)} collective-permute-done((bf16[5248,128]{1,0:T(8,128)(2,1)}, bf16[5248,128]{1,0:T(8,128)(2,1)S(1)}, u32[]{:S(2)}, u32[]{:S(2)}) %collective-permute-start.8) | collective-permute-done | bytes 1343520 | tf_op jit(solution)/shard_map/ppermute | solution.py:37
  106.8 2.7 %add_convert_fusion = bf16[5248,128]{1,0:T(8,128)(2,1)} fusion(bf16[5248,128]{1,0:T(8,128)(2,1)S(1)} %collective-permute-done.8, bf16[5248,128]{1,0:T(8,128)(2,1)} %get-tuple-element.41), kind=kLoop, calls=%fused_computation.2 | loop fusion | flops 2686976 | bytes 4030464 | tf_op jit(solution)/shard_map/convert_element_type | solution.py:449
  109.5 4.4 %all-to-all-start = ((bf16[16,328,128]{2,1,0:T(8,128)(2,1)}), bf16[16,328,128]{2,1,0:T(8,128)(2,1)}, u32[]{:S(2)}, u32[]{:S(2)}) async-start(bf16[16,328,128]{2,1,0:T(8,128)(2,1)} %bitcast.29), calls=%async_computation | async-start | bytes 2686976 | tf_op jit(solution)/shard_map/all_to_all | solution.py:408
  115.9 9.5 %collective-permute-done.10.g2 = bf16[16,104,128]{2,1,0:T(8,128)(2,1)S(1)} collective-permute-done((bf16[16,104,128]{2,1,0:T(8,128)(2,1)}, bf16[16,104,128]{2,1,0:T(8,128)(2,1)S(1)}, u32[]{:S(2)}, u32[]{:S(2)}) %collective-permute-start.10) | collective-permute-done | bytes 426016 | tf_op jit(solution)/shard_map/ppermute | solution.py:37
  125.4 9.9 %collective-permute-done.11.g3 = bf16[16,104,128]{2,1,0:T(8,128)(2,1)S(1)} collective-permute-done((bf16[16,104,128]{2,1,0:T(8,128)(2,1)}, bf16[16,104,128]{2,1,0:T(8,128)(2,1)S(1)}, u32[]{:S(2)}, u32[]{:S(2)}) %collective-permute-start.11) | collective-permute-done | bytes 426016 | tf_op jit(solution)/shard_map/ppermute | solution.py:37
  137.4 4.4 %collective-permute-start.12 = (bf16[8,6656]{1,0:T(8,128)(2,1)S(1)}, bf16[8,6656]{1,0:T(8,128)(2,1)S(1)}, u32[]{:S(2)}, u32[]{:S(2)}) collective-permute-start(bf16[8,6656]{1,0:T(8,128)(2,1)S(1)} %get-tuple-element.47), channel_id=1, source_target_pairs={{0,124},{4,0},{8,4},{12,8},{16,12},{20,16},{24,20},{28,24},{32,28}... | collective-permute-start | bytes 319496 | tf_op jit(solution)/shard_map/ppermute | solution.py:41
  144.5 7.8 %collective-permute-done.13.refs_2_ = bf16[8,6656]{1,0:T(8,128)(2,1)} collective-permute-done((bf16[8,6656]{1,0:T(8,128)(2,1)S(1)}, bf16[8,6656]{1,0:T(8,128)(2,1)}, u32[]{:S(2)}, u32[]{:S(2)}) %collective-permute-start.13) | collective-permute-done | bytes 106528 | tf_op jit(solution)/shard_map/ppermute | solution.py:41
  152.3 2.1 plane_total.1
  154.5 2.4 %collective-permute-start.14 = (bf16[328,128]{1,0:T(8,128)(2,1)}, bf16[328,128]{1,0:T(8,128)(2,1)S(1)}, u32[]{:S(2)}, u32[]{:S(2)}) collective-permute-start(bf16[328,128]{1,0:T(8,128)(2,1)} %plane_total.1), channel_id=1, source_target_pairs={{0,64},{4,68},{8,72},{12,76},{16,80},{20,84},{24,88},{28,92},{32,9... | collective-permute-start | bytes 251912 | tf_op jit(solution)/shard_map/ppermute | solution.py:45
  156.9 10.8 %collective-permute-done.14 = bf16[328,128]{1,0:T(8,128)(2,1)S(1)} collective-permute-done((bf16[328,128]{1,0:T(8,128)(2,1)}, bf16[328,128]{1,0:T(8,128)(2,1)S(1)}, u32[]{:S(2)}, u32[]{:S(2)}) %collective-permute-start.14) | collective-permute-done | bytes 84000 | tf_op jit(solution)/shard_map/ppermute | solution.py:45
  167.8 4.6 %collective-permute-done.16 = bf16[328,128]{1,0:T(8,128)(2,1)S(1)} collective-permute-done((bf16[328,128]{1,0:T(8,128)(2,1)}, bf16[328,128]{1,0:T(8,128)(2,1)S(1)}, u32[]{:S(2)}, u32[]{:S(2)}) %collective-permute-start.16) | collective-permute-done | bytes 84000 | tf_op jit(solution)/shard_map/ppermute | solution.py:489
  174.1 2.1 plane_copies.1
  176.2 6.3 %all-to-all-start.1 = ((bf16[16,328,128]{2,1,0:T(8,128)(2,1)}), bf16[16,328,128]{2,1,0:T(8,128)(2,1)}, u32[]{:S(2)}, u32[]{:S(2)}) async-start(bf16[16,328,128]{2,1,0:T(8,128)(2,1)} %plane_copies.1), calls=%async_computation.1 | async-start | bytes 2686976 | tf_op jit(solution)/shard_map/all_to_all | solution.py:408
  186.1 4.4 %update.1 = bf16[100,64,128]{2,1,0:T(8,128)(2,1)} custom-call(s32[1]{0:T(128)} %bitcast.me_ref.refs_0_, bf16[16,104,128]{2,1,0:T(8,128)(2,1)S(1)} %copy-done.5, bf16[16,104,128]{2,1,0:T(8,128)(2,1)} %collective-permute-done.17.refs_2_.b1, bf16[16,104,128]{2,1,0:T(8,128)(2,1)} %collective-permute-done.18.refs_3_.b2, ...), custom_call_target="tpu_custom_call" | custom-call | bytes 14520000 | tf_op jit(solution)/shard_map/update/pallas_call | solution.py:314
  193.5 10.1 %conv_backward.1 = bf16[100,64,128]{2,1,0:T(8,128)(2,1)} custom-call(s32[1]{0:T(128)} %bitcast.me_ref.refs_0_, bf16[16,104,128]{2,1,0:T(8,128)(2,1)S(1)} %copy-done.6, bf16[16,104,128]{2,1,0:T(8,128)(2,1)S(1)} %copy-done.12, bf16[16,104,128]{2,1,0:T(8,128)(2,1)S(1)} %copy-done.8, bf16[16,104,128]{2,1,0:T(8,128)(2,1)S(1)} %copy-done.10, ...), custom_call_target="tpu_custom_call" | custom-call | bytes 33000000 | tf_op jit(solution)/shard_map/conv_backward/pallas_call | solution.py:158
  203.6 2.4 %collective-permute-start.20 = (bf16[5248,128]{1,0:T(8,128)(2,1)}, bf16[5248,128]{1,0:T(8,128)(2,1)S(1)}, u32[]{:S(2)}, u32[]{:S(2)}) collective-permute-start(bf16[5248,128]{1,0:T(8,128)(2,1)} %bitcast.10.own), channel_id=1, source_target_pairs={{0,1},{1,0},{2,3},{3,2},{4,5},{5,4},{6,7},{7,6},{8,9},{9,8},{10,11... | collective-permute-start | bytes 4030472 | tf_op jit(solution)/shard_map/ppermute | solution.py:37
  206.0 2.9 %collective-permute-done.20.other = bf16[5248,128]{1,0:T(8,128)(2,1)S(1)} collective-permute-done((bf16[5248,128]{1,0:T(8,128)(2,1)}, bf16[5248,128]{1,0:T(8,128)(2,1)S(1)}, u32[]{:S(2)}, u32[]{:S(2)}) %collective-permute-start.20) | collective-permute-done | bytes 1343520 | tf_op jit(solution)/shard_map/ppermute | solution.py:37
  208.9 5.8 %finish.1 = (f32[400,1600]{1,0:T(8,128)}, f32[400,1600]{1,0:T(8,128)}) custom-call(s32[1]{0:T(128)} %bitcast.1.refs_1_.core_ref, bf16[5248,128]{1,0:T(8,128)(2,1)} %bitcast.10.own, bf16[5248,128]{1,0:T(8,128)(2,1)S(1)} %collective-permute-done.20.other, bf16[400,416]{1,0:T(8,128)(2,1)S(1)} %copy-done.4), custom_call_target="tpu_custom_call" | custom-call | bytes 19800000 | tf_op jit(solution)/shard_map/finish/pallas_call | solution.py:473
  (126 shorter events, 47.2 us)
Async XLA Ops:
  4.8 44.2 %collective-permute-start.6 = (bf16[16,104,128]{2,1,0:T(8,128)(2,1)}, bf16[16,104,128]{2,1,0:T(8,128)(2,1)}, u32[]{:S(2)}, u32[]{:S(2)}) collective-permute-start(bf16[16,104,128]{2,1,0:T(8,128)(2,1)} %branch_share.4.refs_0_), channel_id=1, source_target_pairs={{0,2},{1,3},{2,0},{3,1},{4,6},{5,7},{6,4},{7,5},{8,10},{9,11},{10,... | collective-permute-start | bytes 1277960 | tf_op jit(solution)/shard_map/ppermute | solution.py:37
  8.0 54.3 %collective-permute-start.7 = (bf16[16,104,128]{2,1,0:T(8,128)(2,1)}, bf16[16,104,128]{2,1,0:T(8,128)(2,1)}, u32[]{:S(2)}, u32[]{:S(2)}) collective-permute-start(bf16[16,104,128]{2,1,0:T(8,128)(2,1)} %branch_share.5.refs_1_), channel_id=1, source_target_pairs={{0,3},{1,2},{2,1},{3,0},{4,7},{5,6},{6,5},{7,4},{8,11},{9,10},{10,... | collective-permute-start | bytes 1277960 | tf_op jit(solution)/shard_map/ppermute | solution.py:37
  10.3 16.6 %collective-permute-start = (bf16[8,6400]{1,0:T(8,128)(2,1)}, bf16[8,6400]{1,0:T(8,128)(2,1)}, u32[]{:S(2)}, u32[]{:S(2)}) collective-permute-start(bf16[8,6400]{1,0:T(8,128)(2,1)} %get-tuple-element.31), channel_id=1, source_target_pairs={{0,124},{4,0},{8,4},{12,8},{16,12},{20,16},{24,20},{28,24},{32,28}... | collective-permute-start | bytes 307208 | tf_op jit(solution)/shard_map/ppermute | solution.py:41
  19.0 16.7 %collective-permute-start.1 = (bf16[8,6400]{1,0:T(8,128)(2,1)S(1)}, bf16[8,6400]{1,0:T(8,128)(2,1)}, u32[]{:S(2)}, u32[]{:S(2)}) collective-permute-start(bf16[8,6400]{1,0:T(8,128)(2,1)S(1)} %get-tuple-element.32), channel_id=1, source_target_pairs={{0,4},{4,8},{8,12},{12,16},{16,20},{20,24},{24,28},{28,32},{32,36}... | collective-permute-start | bytes 307208 | tf_op jit(solution)/shard_map/ppermute | solution.py:41
  20.2 42.1 %collective-permute-start.5 = (bf16[16,104,128]{2,1,0:T(8,128)(2,1)}, bf16[16,104,128]{2,1,0:T(8,128)(2,1)}, u32[]{:S(2)}, u32[]{:S(2)}) collective-permute-start(bf16[16,104,128]{2,1,0:T(8,128)(2,1)} %branch_share.7), channel_id=1, source_target_pairs={{0,1},{1,0},{2,3},{3,2},{4,5},{5,4},{6,7},{7,6},{8,9},{9,8},{10,11... | collective-permute-start | bytes 1277960 | tf_op jit(solution)/shard_map/ppermute | solution.py:37
  47.1 15.2 %collective-permute-start.2 = (bf16[16,104,128]{2,1,0:T(8,128)(2,1)}, bf16[16,104,128]{2,1,0:T(8,128)(2,1)}, u32[]{:S(2)}, u32[]{:S(2)}) collective-permute-start(bf16[16,104,128]{2,1,0:T(8,128)(2,1)} %get-tuple-element.34), channel_id=1, source_target_pairs={{0,1},{1,0},{2,3},{3,2},{4,5},{5,4},{6,7},{7,6},{8,9},{9,8},{10,11... | collective-permute-start | bytes 1277960 | tf_op jit(solution)/shard_map/ppermute | solution.py:37
  49.0 13.4 %collective-permute-start.3 = (bf16[16,104,128]{2,1,0:T(8,128)(2,1)}, bf16[16,104,128]{2,1,0:T(8,128)(2,1)}, u32[]{:S(2)}, u32[]{:S(2)}) collective-permute-start(bf16[16,104,128]{2,1,0:T(8,128)(2,1)} %get-tuple-element.35), channel_id=1, source_target_pairs={{0,2},{1,3},{2,0},{3,1},{4,6},{5,7},{6,4},{7,5},{8,10},{9,11},{10,... | collective-permute-start | bytes 1277960 | tf_op jit(solution)/shard_map/ppermute | solution.py:37
  49.0 21.0 %collective-permute-start.4 = (bf16[16,104,128]{2,1,0:T(8,128)(2,1)}, bf16[16,104,128]{2,1,0:T(8,128)(2,1)}, u32[]{:S(2)}, u32[]{:S(2)}) collective-permute-start(bf16[16,104,128]{2,1,0:T(8,128)(2,1)} %get-tuple-element.36), channel_id=1, source_target_pairs={{0,3},{1,2},{2,1},{3,0},{4,7},{5,6},{6,5},{7,4},{8,11},{9,10},{10,... | collective-permute-start | bytes 1277960 | tf_op jit(solution)/shard_map/ppermute | solution.py:37
  103.4 3.4 %collective-permute-start.8 = (bf16[5248,128]{1,0:T(8,128)(2,1)}, bf16[5248,128]{1,0:T(8,128)(2,1)S(1)}, u32[]{:S(2)}, u32[]{:S(2)}) collective-permute-start(bf16[5248,128]{1,0:T(8,128)(2,1)} %get-tuple-element.42), channel_id=1, source_target_pairs={{0,1},{1,0},{2,3},{3,2},{4,5},{5,4},{6,7},{7,6},{8,9},{9,8},{10,11... | collective-permute-start | bytes 4030472 | tf_op jit(solution)/shard_map/ppermute | solution.py:37
  109.5 42.8 %all-to-all-start = ((bf16[16,328,128]{2,1,0:T(8,128)(2,1)}), bf16[16,328,128]{2,1,0:T(8,128)(2,1)}, u32[]{:S(2)}, u32[]{:S(2)}) async-start(bf16[16,328,128]{2,1,0:T(8,128)(2,1)} %bitcast.29), calls=%async_computation | async-start | bytes 2686976 | tf_op jit(solution)/shard_map/all_to_all | solution.py:408
  113.9 11.5 %collective-permute-start.10 = (bf16[16,104,128]{2,1,0:T(8,128)(2,1)}, bf16[16,104,128]{2,1,0:T(8,128)(2,1)S(1)}, u32[]{:S(2)}, u32[]{:S(2)}) collective-permute-start(bf16[16,104,128]{2,1,0:T(8,128)(2,1)} %get-tuple-element.45), channel_id=1, source_target_pairs={{0,2},{1,3},{2,0},{3,1},{4,6},{5,7},{6,4},{7,5},{8,10},{9,11},{10,... | collective-permute-start | bytes 1277960 | tf_op jit(solution)/shard_map/ppermute | solution.py:37
  114.0 21.3 %collective-permute-start.11 = (bf16[16,104,128]{2,1,0:T(8,128)(2,1)}, bf16[16,104,128]{2,1,0:T(8,128)(2,1)S(1)}, u32[]{:S(2)}, u32[]{:S(2)}) collective-permute-start(bf16[16,104,128]{2,1,0:T(8,128)(2,1)} %get-tuple-element.46), channel_id=1, source_target_pairs={{0,3},{1,2},{2,1},{3,0},{4,7},{5,6},{6,5},{7,4},{8,11},{9,10},{10,... | collective-permute-start | bytes 1277960 | tf_op jit(solution)/shard_map/ppermute | solution.py:37
  115.9 19.4 %collective-permute-start.9 = (bf16[16,104,128]{2,1,0:T(8,128)(2,1)}, bf16[16,104,128]{2,1,0:T(8,128)(2,1)S(1)}, u32[]{:S(2)}, u32[]{:S(2)}) collective-permute-start(bf16[16,104,128]{2,1,0:T(8,128)(2,1)} %get-tuple-element.44), channel_id=1, source_target_pairs={{0,1},{1,0},{2,3},{3,2},{4,5},{5,4},{6,7},{7,6},{8,9},{9,8},{10,11... | collective-permute-start | bytes 1277960 | tf_op jit(solution)/shard_map/ppermute | solution.py:37
  137.4 7.1 %collective-permute-start.12 = (bf16[8,6656]{1,0:T(8,128)(2,1)S(1)}, bf16[8,6656]{1,0:T(8,128)(2,1)S(1)}, u32[]{:S(2)}, u32[]{:S(2)}) collective-permute-start(bf16[8,6656]{1,0:T(8,128)(2,1)S(1)} %get-tuple-element.47), channel_id=1, source_target_pairs={{0,124},{4,0},{8,4},{12,8},{16,12},{20,16},{24,20},{28,24},{32,28}... | collective-permute-start | bytes 319496 | tf_op jit(solution)/shard_map/ppermute | solution.py:41
  141.8 10.5 %collective-permute-start.13 = (bf16[8,6656]{1,0:T(8,128)(2,1)S(1)}, bf16[8,6656]{1,0:T(8,128)(2,1)}, u32[]{:S(2)}, u32[]{:S(2)}) collective-permute-start(bf16[8,6656]{1,0:T(8,128)(2,1)S(1)} %get-tuple-element.48), channel_id=1, source_target_pairs={{0,4},{4,8},{8,12},{12,16},{16,20},{20,24},{24,28},{28,32},{32,36}... | collective-permute-start | bytes 319496 | tf_op jit(solution)/shard_map/ppermute | solution.py:41
  141.8 32.2 %collective-permute-start.17 = (bf16[16,104,128]{2,1,0:T(8,128)(2,1)}, bf16[16,104,128]{2,1,0:T(8,128)(2,1)}, u32[]{:S(2)}, u32[]{:S(2)}) collective-permute-start(bf16[16,104,128]{2,1,0:T(8,128)(2,1)} %get-tuple-element.50), channel_id=1, source_target_pairs={{0,1},{1,0},{2,3},{3,2},{4,5},{5,4},{6,7},{7,6},{8,9},{9,8},{10,11... | collective-permute-start | bytes 1277960 | tf_op jit(solution)/shard_map/ppermute | solution.py:37
  141.8 32.2 %collective-permute-start.18 = (bf16[16,104,128]{2,1,0:T(8,128)(2,1)}, bf16[16,104,128]{2,1,0:T(8,128)(2,1)}, u32[]{:S(2)}, u32[]{:S(2)}) collective-permute-start(bf16[16,104,128]{2,1,0:T(8,128)(2,1)} %get-tuple-element.51), channel_id=1, source_target_pairs={{0,2},{1,3},{2,0},{3,1},{4,6},{5,7},{6,4},{7,5},{8,10},{9,11},{10,... | collective-permute-start | bytes 1277960 | tf_op jit(solution)/shard_map/ppermute | solution.py:37
  142.1 32.0 %collective-permute-start.19 = (bf16[16,104,128]{2,1,0:T(8,128)(2,1)}, bf16[16,104,128]{2,1,0:T(8,128)(2,1)}, u32[]{:S(2)}, u32[]{:S(2)}) collective-permute-start(bf16[16,104,128]{2,1,0:T(8,128)(2,1)} %get-tuple-element.52), channel_id=1, source_target_pairs={{0,3},{1,2},{2,1},{3,0},{4,7},{5,6},{6,5},{7,4},{8,11},{9,10},{10,... | collective-permute-start | bytes 1277960 | tf_op jit(solution)/shard_map/ppermute | solution.py:37
  154.5 13.2 %collective-permute-start.14 = (bf16[328,128]{1,0:T(8,128)(2,1)}, bf16[328,128]{1,0:T(8,128)(2,1)S(1)}, u32[]{:S(2)}, u32[]{:S(2)}) collective-permute-start(bf16[328,128]{1,0:T(8,128)(2,1)} %plane_total.1), channel_id=1, source_target_pairs={{0,64},{4,68},{8,72},{12,76},{16,80},{20,84},{24,88},{28,92},{32,9... | collective-permute-start | bytes 251912 | tf_op jit(solution)/shard_map/ppermute | solution.py:45
  156.9 10.9 %collective-permute-start.15 = (bf16[328,128]{1,0:T(8,128)(2,1)}, bf16[328,128]{1,0:T(8,128)(2,1)S(1)}, u32[]{:S(2)}, u32[]{:S(2)}) collective-permute-start(bf16[328,128]{1,0:T(8,128)(2,1)} %plane_total.1), channel_id=1, source_target_pairs={{0,2},{1,3},{2,0},{3,1},{4,6},{5,7},{6,4},{7,5},{8,10},{9,11},{10,... | collective-permute-start | bytes 251912 | tf_op jit(solution)/shard_map/ppermute | solution.py:37
  167.7 4.7 %collective-permute-start.16 = (bf16[328,128]{1,0:T(8,128)(2,1)}, bf16[328,128]{1,0:T(8,128)(2,1)S(1)}, u32[]{:S(2)}, u32[]{:S(2)}) collective-permute-start(bf16[328,128]{1,0:T(8,128)(2,1)} %plane_total.1), channel_id=1, source_target_pairs={{0,66},{1,67},{2,64},{3,65},{4,70},{5,71},{6,68},{7,69},{8,74},{9,... | collective-permute-start | bytes 251912 | tf_op jit(solution)/shard_map/ppermute | solution.py:489
  176.2 27.4 %all-to-all-start.1 = ((bf16[16,328,128]{2,1,0:T(8,128)(2,1)}), bf16[16,328,128]{2,1,0:T(8,128)(2,1)}, u32[]{:S(2)}, u32[]{:S(2)}) async-start(bf16[16,328,128]{2,1,0:T(8,128)(2,1)} %plane_copies.1), calls=%async_computation.1 | async-start | bytes 2686976 | tf_op jit(solution)/shard_map/all_to_all | solution.py:408
  193.5 15.5 %copy-start.4 = (bf16[400,416]{1,0:T(8,128)(2,1)S(1)}, bf16[400,416]{1,0:T(8,128)(2,1)}, u32[]{:S(2)}) copy-start(bf16[400,416]{1,0:T(8,128)(2,1)} %copy-done.3) | copy-start | bytes 998404
  203.6 5.3 %collective-permute-start.20 = (bf16[5248,128]{1,0:T(8,128)(2,1)}, bf16[5248,128]{1,0:T(8,128)(2,1)S(1)}, u32[]{:S(2)}, u32[]{:S(2)}) collective-permute-start(bf16[5248,128]{1,0:T(8,128)(2,1)} %bitcast.10.own), channel_id=1, source_target_pairs={{0,1},{1,0},{2,3},{3,2},{4,5},{5,4},{6,7},{7,6},{8,9},{9,8},{10,11... | collective-permute-start | bytes 4030472 | tf_op jit(solution)/shard_map/ppermute | solution.py:37
  (30 other events, 124.1 us)

commit v3 on v2

--- a/solution.py
+++ b/solution.py
@@ -45,7 +45,8 @@
     return lax.ppermute(x, "lon", [(i, i ^ k) for i in range(32)])
 
 
-def share_kernel(me_ref, cot_ref, mask_ref, scale_ref, out_ref):
+def share_kernel(me_ref, cot_ref, mask_ref, scale_ref, *refs):
+    out_ref = refs[-1]
     cells = cot_ref[...].astype(F32)
     cells = jnp.concatenate([cells, jnp.zeros((CP - LC, QR, LANES), F32)], axis=0)
     cells = jnp.swapaxes(cells, 0, 1)
@@ -53,7 +54,7 @@
     out_ref[...] = ((cells * mask[:, None, :]) * scale_ref[...][None]).astype(BF)
 
 
-def branch_share(me, cotangent, sea_mask, scale, k):
+def branch_share(me, cotangent, sea_mask, scale, k, after):
     return pl.pallas_call(
         share_kernel,
         out_shape=jax.ShapeDtypeStruct((QR, CP, LANES), BF),
@@ -64,13 +65,14 @@
                 pl.BlockSpec((LC, QR, LANES), lambda i, me: (0, me[0] ^ k, 0)),
                 pl.BlockSpec((QR, LANES), lambda i, me: (me[0] ^ k, 0)),
                 pl.BlockSpec((CP, 1), lambda i, me: (0, 0)),
-            ],
+            ]
+            + [pl.BlockSpec(memory_space=pl.ANY)] * len(after),
             out_specs=pl.BlockSpec((QR, CP, LANES), lambda i, me: (0, 0, 0)),
         ),
         compiler_params=pltpu.CompilerParams(vmem_limit_bytes=32 << 20),
         cost_estimate=cost(1.2),
         name="branch_share",
-    )(me, cotangent, sea_mask, scale)
+    )(me, cotangent, sea_mask, scale, *after)
 
 
 def conv_channel(cells, rim, pattern, lane, band):
@@ -372,33 +374,26 @@
     return head, tail
 
 
-def edges_kernel(cells, pick, *refs):
-    both = dotg(pick[...], cells[...], 1, 1)
-    refs[-2][...] = both[:8].astype(BF)
-    refs[-1][...] = both[8:].astype(BF)
-
-
-def edges(cells2d, picks, after=()):
+def edge_kernel(cells, pick, *refs):
+    refs[-1][...] = dotg(pick[...], cells[...], 1, 1).astype(BF)
+
+
+def edge(cells2d, pick, after=()):
     vmem = pl.BlockSpec(memory_space=pltpu.VMEM)
-    out = jax.ShapeDtypeStruct((8, cells2d.shape[0]), BF)
-    return pl.pallas_call(
-        edges_kernel,
-        out_shape=[out, out],
+    return pl.pallas_call(
+        edge_kernel,
+        out_shape=jax.ShapeDtypeStruct((8, cells2d.shape[0]), BF),
         in_specs=[vmem, vmem] + [pl.BlockSpec(memory_space=pl.ANY)] * len(after),
-        out_specs=[vmem, vmem],
+        out_specs=vmem,
         compiler_params=pltpu.CompilerParams(vmem_limit_bytes=32 << 20),
-        cost_estimate=cost(1.5),
-        name="edges",
-    )(cells2d, picks, *after)
-
-
-def rims(cells2d, after=()):
-    picks = jnp.concatenate(edge_picks(), 0)
-    first, last = edges(cells2d, picks, after)
-    from_right = lon_shift(first, -1)
-    from_left = lon_shift(last, 1)
-    both = [from_right, from_left]
-    return dotg(jnp.concatenate(both, 0), picks, 0, 0).astype(BF), both
+        cost_estimate=cost(1),
+        name="edge",
+    )(cells2d, pick, *after)
+
+
+def rims(first, last):
+    both = jnp.concatenate([lon_shift(first, -1), lon_shift(last, 1)], 0)
+    return dotg(both, jnp.concatenate(edge_picks(), 0), 0, 0).astype(BF)
 
 
 PLANES = [[16 * half + i for i in range(16)] for half in range(2)]
@@ -427,32 +422,32 @@
     )(pieces, *after)
 
 
-def copies_kernel(*refs):
+def copies_kernel(part, out):
     for i in range(16):
-        refs[-1][i] = refs[0][...]
-
-
-def plane_copies(part, after):
+        out[i] = part[...]
+
+
+def plane_copies(part):
     vmem = pl.BlockSpec(memory_space=pltpu.VMEM)
     return pl.pallas_call(
         copies_kernel,
         out_shape=jax.ShapeDtypeStruct((16, PIECE, LANES), BF),
-        in_specs=[vmem] + [pl.BlockSpec(memory_space=pl.ANY)] * len(after),
+        in_specs=[vmem],
         out_specs=vmem,
         cost_estimate=cost(1),
         name="plane_copies",
-    )(part, *after)
-
-
-def reduce_gradients(keep, send, early, late):
+    )(part)
+
+
+def reduce_gradients(keep, send, after):
     mine = keep.astype(F32) + ch_swap(send, 1).astype(F32)
     mine = plane_exchange(mine.astype(BF).reshape(16, PIECE, LANES))
-    wire = plane_total(mine, early)
+    wire = plane_total(mine, after)
     part = (
         (wire.astype(F32) + lon_swap(wire, 16).astype(F32))
         + (ch_swap(wire, 2).astype(F32) + both_swap(wire).astype(F32))
     ).astype(BF)
-    return plane_exchange(plane_copies(part, late)).reshape(WIRE, LANES)
+    return plane_exchange(plane_copies(part)).reshape(WIRE, LANES)
 
 
 def finish_kernel(core_ref, own, other, pad, grad_in, grad_out, held):
@@ -508,7 +503,15 @@
     core = (ch & 1).reshape(1)
     scale = jnp.pad(layer_scale, (0, CP - LC)).reshape(CP, 1)
 
-    sent = {k: branch_share(me, cotangent, sea_mask, scale, k) for k in (2, 3, 1, 0)}
+    head, tail = edge_picks()
+    state2d = ocean_state.reshape(LC * ROWS, LANES)
+    sent = {}
+    first = edge(state2d, head)
+    sent[2] = branch_share(me, cotangent, sea_mask, scale, 2, (first,))
+    last = edge(state2d, tail, (sent[2],))
+    sent[3] = branch_share(me, cotangent, sea_mask, scale, 3, (last,))
+    sent[1] = branch_share(me, cotangent, sea_mask, scale, 1, (sent[3],))
+    sent[0] = branch_share(me, cotangent, sea_mask, scale, 0, (sent[1],))
     gs = [sent[0]] + [ch_swap(sent[k], k) for k in (1, 2, 3)]
 
     chan = jnp.arange(C)
@@ -517,8 +520,7 @@
     vec = jnp.stack([norm_gain, norm_bias, bias_out], 1).reshape(4, LC, 3)
     vec = jnp.pad(vec, ((0, 0), (0, CP - LC), (0, 0))).reshape(4 * CP, 3)
 
-    state_rim, _ = rims(ocean_state.reshape(LC * ROWS, LANES), (sent[2], sent[3]))
-    state_rim = state_rim.reshape(LC, ROWS, LANES)
+    state_rim = rims(first, last).reshape(LC, ROWS, LANES)
     bias = jnp.broadcast_to(conv_bias[:, None, None], (LC, 1, LANES))
     conv = conv_forward(me, ocean_state, state_rim, tap_patterns(kernel), bias)
     xs = [conv[0]] + [ch_swap(conv[k], k) for k in (1, 2, 3)]
@@ -531,9 +533,8 @@
     pieces = [branch[0]] + [ch_swap(branch[k], k) for k in (1, 2, 3)]
 
     every = jnp.concatenate(grads, 0).reshape(4 * QR * CP, LANES)
-    grad_rims, arrived = rims(every)
-    grad_rims = grad_rims.reshape(4, QR, CP, LANES)
-    own = reduce_gradients(keep, send, arrived, pieces)
+    grad_rims = rims(edge(every, head), edge(every, tail)).reshape(4, QR, CP, LANES)
+    own = reduce_gradients(keep, send, grads[1:] + pieces[1:])
 
     grad_state = conv_backward(
         me,

time: 216 us -> 214 us (level)
  waiting for transfers between devices: 67 us -> 55.5 us
  starting transfers between devices: 39.9 us -> 46.3 us
  Pallas kernels: 76 us -> 78.8 us
    ppermute x15, waiting for transfers between devices: 32.9 us -> 50 us  [ch_swap(): return lax.ppermute(x, 'ch', [(i, i ^ k) for i in range(4)])]
    ppermute x4, waiting for transfers between devices: 18.6 us -> 2.56 us  [lon_shift(): return lax.ppermute(x, 'lon', [(i, (i + d) % 32) for i in range(32)])]
    ppermute x1, waiting for transfers between devices: 10.8 us -> 1.99 us  [lon_swap(): return lax.ppermute(x, 'lon', [(i, i ^ k) for i in range(32)])]
    ppermute x4, starting transfers between devices: 13.2 us -> 16.9 us  [lon_shift(): return lax.ppermute(x, 'lon', [(i, (i + d) % 32) for i in range(32)])]
    ppermute x1, waiting for transfers between devices: 4.62 us -> 0.94 us  [both_swap(): lax.ppermute(x, ('lon', 'ch'), [(i, i ^ 16 * 4 + 2) for i in range(128)])]
    unnamed x63 -> x47, local copies, waits for them, and re-layouts: 12.5 us -> 12.2 us
  transfers between devices with their start and end apart: 23 -> 23, of which waited for: 11 -> 12; matrix products, arithmetic and copies ran while one was open for 7% -> 7% of each run, Pallas kernels for 16% -> 16%
where the time goes in v3:
time: 214 us; the launch traced here: 212 us
  Pallas kernels  78.8 us (37%)
  waiting for transfers between devices  55.5 us (26%)
  starting transfers between devices  46.3 us (22%)
  local copies, waits for them, and re-layouts  19.7 us (9%)
  other arithmetic  6.19 us (3%)
  matrix products  4.98 us (2%)
    ppermute x15, waiting for transfers between devices, ch_swap(): return lax.ppermute(x, 'ch', [(i, i ^ k) for i in range(4)])  50 us
    pallas_call x1, Pallas kernels, mlp(): pl.pallas_call(mlp_kernel, out_shape=[share] * 8 + [jax.ShapeDtypeStruct(...  33.5 us
    ppermute x4, starting transfers between devices, lon_shift(): return lax.ppermute(x, 'lon', [(i, (i + d) % 32) for i in range(32)])  16.9 us
    ppermute x15, starting transfers between devices, ch_swap(): return lax.ppermute(x, 'ch', [(i, i ^ k) for i in range(4)])  14.2 us
    unnamed x47, local copies, waits for them, and re-layouts  12.2 us
    all_to_all x2, starting transfers between devices, plane_exchange(): return lax.all_to_all(pieces, 'lon', 0, 0, axis_index_groups=PLANES)  11.2 us
    pallas_call x1, Pallas kernels, conv_backward(): pl.pallas_call(backward_kernel, out_shape=jax.ShapeDtypeStruct((LC, ROWS,...  11.1 us
    pallas_call x1, Pallas kernels, conv_forward(): pl.pallas_call(forward_kernel, out_shape=[share] * 4, grid_spec=pltpu.Pre...  8.84 us
  transfers between devices with their start and end apart: 23, of which 12 were waited for; matrix products, arithmetic and copies ran while one was open for 7% of the time, Pallas kernels for 16%

profile of v3, /device:TPU:1, one launch (start us, length us, event | category | flops | bytes accessed | tf_op | source)
XLA Modules:
  0.0 212.3 jit_solution(9688369423422155531)
XLA Ops:
  2.8 9.5 %collective-permute-start = (bf16[8,6400]{1,0:T(8,128)(2,1)S(1)}, bf16[8,6400]{1,0:T(8,128)(2,1)}, u32[]{:S(2)}, u32[]{:S(2)}) collective-permute-start(bf16[8,6400]{1,0:T(8,128)(2,1)S(1)} %edge.4.refs_0_), channel_id=1, source_target_pairs={{0,124},{4,0},{8,4},{12,8},{16,12},{20,16},{24,20},{28,24},{32,28}... | collective-permute-start | bytes 307208 | tf_op jit(solution)/shard_map/ppermute | solution.py:41
  17.8 2.3 %collective-permute-start.7 = (bf16[16,104,128]{2,1,0:T(8,128)(2,1)}, bf16[16,104,128]{2,1,0:T(8,128)(2,1)}, u32[]{:S(2)}, u32[]{:S(2)}) collective-permute-start(bf16[16,104,128]{2,1,0:T(8,128)(2,1)} %branch_share.5.refs_0_), channel_id=1, source_target_pairs={{0,3},{1,2},{2,1},{3,0},{4,7},{5,6},{6,5},{7,4},{8,11},{9,10},{10,... | collective-permute-start | bytes 1277960 | tf_op jit(solution)/shard_map/ppermute | solution.py:37
  29.4 8.8 %conv_forward.1 = (bf16[16,104,128]{2,1,0:T(8,128)(2,1)S(1)}, bf16[16,104,128]{2,1,0:T(8,128)(2,1)}, bf16[16,104,128]{2,1,0:T(8,128)(2,1)}, bf16[16,104,128]{2,1,0:T(8,128)(2,1)}) custom-call(s32[1]{0:T(128)} %bitcast.me_ref.refs_0_, bf16[100,64,128]{2,1,0:T(8,128)(2,1)S(1)} %copy-done.2, bf16[100,64,128]{2,1,0:T(8,128)(2,1)S(1)} %bitcast.25, ...), custom_call_target="tpu_custom_call" | custom-call | bytes 29700000 | tf_op jit(solution)/shard_map/conv_forward/pallas_call | solution.py:121
  39.0 2.2 %collective-permute-start.2 = (bf16[16,104,128]{2,1,0:T(8,128)(2,1)}, bf16[16,104,128]{2,1,0:T(8,128)(2,1)}, u32[]{:S(2)}, u32[]{:S(2)}) collective-permute-start(bf16[16,104,128]{2,1,0:T(8,128)(2,1)} %get-tuple-element.28), channel_id=1, source_target_pairs={{0,1},{1,0},{2,3},{3,2},{4,5},{5,4},{6,7},{7,6},{8,9},{9,8},{10,11... | collective-permute-start | bytes 1277960 | tf_op jit(solution)/shard_map/ppermute | solution.py:37
  48.1 3.5 %padded_weights.1 = (bf16[416,1600]{1,0:T(8,128)(2,1)S(1)}, bf16[1600,416]{1,0:T(8,128)(2,1)}, bf16[416,1600]{1,0:T(8,128)(2,1)S(1)}, bf16[1600,416]{1,0:T(8,128)(2,1)}) custom-call(bf16[400,1600]{1,0:T(8,128)(2,1)S(1)} %copy-done.9, bf16[400,1600]{1,0:T(8,128)(2,1)S(1)} %bitcast.30, bf16[400,416]{1,0:T(8,128)(2,1)S(1)} %fusion.pad), custom_call_target="tpu_custom_call" | custom-call | bytes 16500000 | tf_op jit(solution)/shard_map/padded_weights/pallas_call | solution.py:347
  54.5 7.6 %collective-permute-done.4.refs_5_ = bf16[16,104,128]{2,1,0:T(8,128)(2,1)} collective-permute-done((bf16[16,104,128]{2,1,0:T(8,128)(2,1)}, bf16[16,104,128]{2,1,0:T(8,128)(2,1)}, u32[]{:S(2)}, u32[]{:S(2)}) %collective-permute-start.4) | collective-permute-done | bytes 426016 | tf_op jit(solution)/shard_map/ppermute | solution.py:37
  62.1 33.5 %mlp.1 = (bf16[16,104,128]{2,1,0:T(8,128)(2,1)}, bf16[16,104,128]{2,1,0:T(8,128)(2,1)}, bf16[16,104,128]{2,1,0:T(8,128)(2,1)}, bf16[16,104,128]{2,1,0:T(8,128)(2...) custom-call(s32[1]{0:T(128)} %bitcast.me_ref.refs_0_, ...), custom_call_target="tpu_custom_call" | custom-call | bytes 112200000 | tf_op jit(solution)/shard_map/mlp/pallas_call | solution.py:270
  96.0 3.0 %collective-permute-done.8 = bf16[5248,128]{1,0:T(8,128)(2,1)S(1)} collective-permute-done((bf16[5248,128]{1,0:T(8,128)(2,1)}, bf16[5248,128]{1,0:T(8,128)(2,1)S(1)}, u32[]{:S(2)}, u32[]{:S(2)}) %collective-permute-start.8) | collective-permute-done | bytes 1343520 | tf_op jit(solution)/shard_map/ppermute | solution.py:37
  99.0 2.7 %add_convert_fusion = bf16[5248,128]{1,0:T(8,128)(2,1)} fusion(bf16[5248,128]{1,0:T(8,128)(2,1)S(1)} %collective-permute-done.8, bf16[5248,128]{1,0:T(8,128)(2,1)} %get-tuple-element.35), kind=kLoop, calls=%fused_computation.2 | loop fusion | flops 2686976 | bytes 4030464 | tf_op jit(solution)/shard_map/convert_element_type | solution.py:444
  101.7 4.4 %all-to-all-start = ((bf16[16,328,128]{2,1,0:T(8,128)(2,1)}), bf16[16,328,128]{2,1,0:T(8,128)(2,1)}, u32[]{:S(2)}, u32[]{:S(2)}) async-start(bf16[16,328,128]{2,1,0:T(8,128)(2,1)} %bitcast.31), calls=%async_computation | async-start | bytes 2686976 | tf_op jit(solution)/shard_map/all_to_all | solution.py:403
  110.2 7.9 %collective-permute-done.13.refs_5_.b2 = bf16[16,104,128]{2,1,0:T(8,128)(2,1)} collective-permute-done((bf16[16,104,128]{2,1,0:T(8,128)(2,1)}, bf16[16,104,128]{2,1,0:T(8,128)(2,1)}, u32[]{:S(2)}, u32[]{:S(2)}) %collective-permute-start.13) | collective-permute-done | bytes 426016 | tf_op jit(solution)/shard_map/ppermute | solution.py:37
  118.1 10.3 %collective-permute-done.14.refs_6_.b3 = bf16[16,104,128]{2,1,0:T(8,128)(2,1)} collective-permute-done((bf16[16,104,128]{2,1,0:T(8,128)(2,1)}, bf16[16,104,128]{2,1,0:T(8,128)(2,1)}, u32[]{:S(2)}, u32[]{:S(2)}) %collective-permute-start.14) | collective-permute-done | bytes 426016 | tf_op jit(solution)/shard_map/ppermute | solution.py:37
  128.4 7.9 %collective-permute-done.10.refs_2_.g2 = bf16[16,104,128]{2,1,0:T(8,128)(2,1)} collective-permute-done((bf16[16,104,128]{2,1,0:T(8,128)(2,1)}, bf16[16,104,128]{2,1,0:T(8,128)(2,1)}, u32[]{:S(2)}, u32[]{:S(2)}) %collective-permute-start.10) | collective-permute-done | bytes 426016 | tf_op jit(solution)/shard_map/ppermute | solution.py:37
  136.3 9.4 %collective-permute-done.11.refs_3_.g3 = bf16[16,104,128]{2,1,0:T(8,128)(2,1)} collective-permute-done((bf16[16,104,128]{2,1,0:T(8,128)(2,1)}, bf16[16,104,128]{2,1,0:T(8,128)(2,1)}, u32[]{:S(2)}, u32[]{:S(2)}) %collective-permute-start.11) | collective-permute-done | bytes 426016 | tf_op jit(solution)/shard_map/ppermute | solution.py:37
  145.8 2.1 %plane_total.1 = bf16[328,128]{1,0:T(8,128)(2,1)} custom-call(bf16[16,328,128]{2,1,0:T(8,128)(2,1)} %all-to-all-done.refs_0_, bf16[16,104,128]{2,1,0:T(8,128)(2,1)} %collective-permute-done.9.refs_1_.g1, bf16[16,104,128]{2,1,0:T(8,128)(2,1)} %collective-permute-done.10.refs_2_.g2, bf16[16,104,128]{2,1,0:T(8,128)(2,1)} %collective-permute-done.11.refs_3_.g3, ...), custom_call_target="tpu_custom_call" | custom-call | bytes 3960000 | tf_op jit(solution)/shard_map/plane_total/pallas_call | solution.py:415
  147.9 3.0 %collective-permute-start.15 = (bf16[328,128]{1,0:T(8,128)(2,1)}, bf16[328,128]{1,0:T(8,128)(2,1)S(1)}, u32[]{:S(2)}, u32[]{:S(2)}) collective-permute-start(bf16[328,128]{1,0:T(8,128)(2,1)} %plane_total.1), channel_id=1, source_target_pairs={{0,64},{4,68},{8,72},{12,76},{16,80},{20,84},{24,88},{28,92},{32,9... | collective-permute-start | bytes 251912 | tf_op jit(solution)/shard_map/ppermute | solution.py:45
  157.3 2.1 %plane_copies.1 = bf16[16,328,128]{2,1,0:T(8,128)(2,1)} custom-call(bf16[328,128]{1,0:T(8,128)(2,1)} %add_convert_fusion.1.part), custom_call_target="tpu_custom_call" | custom-call | bytes 3300000 | tf_op jit(solution)/shard_map/plane_copies/pallas_call | solution.py:432
  159.4 6.9 %all-to-all-start.1 = ((bf16[16,328,128]{2,1,0:T(8,128)(2,1)}), bf16[16,328,128]{2,1,0:T(8,128)(2,1)}, u32[]{:S(2)}, u32[]{:S(2)}) async-start(bf16[16,328,128]{2,1,0:T(8,128)(2,1)} %plane_copies.1), calls=%async_computation.1 | async-start | bytes 2686976 | tf_op jit(solution)/shard_map/all_to_all | solution.py:403
  169.6 7.4 %collective-permute-start.18 = (bf16[8,6656]{1,0:T(8,128)(2,1)}, bf16[8,6656]{1,0:T(8,128)(2,1)}, u32[]{:S(2)}, u32[]{:S(2)}) collective-permute-start(bf16[8,6656]{1,0:T(8,128)(2,1)} %edge.6), channel_id=1, source_target_pairs={{0,124},{4,0},{8,4},{12,8},{16,12},{20,16},{24,20},{28,24},{32,28}... | collective-permute-start | bytes 319496 | tf_op jit(solution)/shard_map/ppermute | solution.py:41
  180.6 4.4 %update.1 = bf16[100,64,128]{2,1,0:T(8,128)(2,1)} custom-call(s32[1]{0:T(128)} %bitcast.me_ref.refs_0_, bf16[16,104,128]{2,1,0:T(8,128)(2,1)S(1)} %copy-done.15, bf16[16,104,128]{2,1,0:T(8,128)(2,1)} %collective-permute-done.12.refs_4_.b1, bf16[16,104,128]{2,1,0:T(8,128)(2,1)} %collective-permute-done.13.refs_5_.b2, ...), custom_call_target="tpu_custom_call" | custom-call | bytes 14520000 | tf_op jit(solution)/shard_map/update/pallas_call | solution.py:316
  189.2 11.1 %conv_backward.1 = bf16[100,64,128]{2,1,0:T(8,128)(2,1)} custom-call(s32[1]{0:T(128)} %bitcast.me_ref.refs_0_, bf16[16,104,128]{2,1,0:T(8,128)(2,1)S(1)} %copy-done.5, bf16[16,104,128]{2,1,0:T(8,128)(2,1)} %collective-permute-done.9.refs_1_.g1, bf16[16,104,128]{2,1,0:T(8,128)(2,1)} %collective-permute-done.10.refs_2_.g2, ...), custom_call_target="tpu_custom_call" | custom-call | bytes 33000000 | tf_op jit(solution)/shard_map/conv_backward/pallas_call | solution.py:160
  200.3 3.4 %collective-permute-start.20 = (bf16[5248,128]{1,0:T(8,128)(2,1)}, bf16[5248,128]{1,0:T(8,128)(2,1)S(1)}, u32[]{:S(2)}, u32[]{:S(2)}) collective-permute-start(bf16[5248,128]{1,0:T(8,128)(2,1)} %bitcast.9.own), channel_id=1, source_target_pairs={{0,1},{1,0},{2,3},{3,2},{4,5},{5,4},{6,7},{7,6},{8,9},{9,8},{10,11... | collective-permute-start | bytes 4030472 | tf_op jit(solution)/shard_map/ppermute | solution.py:37
  203.6 2.9 %collective-permute-done.20.other = bf16[5248,128]{1,0:T(8,128)(2,1)S(1)} collective-permute-done((bf16[5248,128]{1,0:T(8,128)(2,1)}, bf16[5248,128]{1,0:T(8,128)(2,1)S(1)}, u32[]{:S(2)}, u32[]{:S(2)}) %collective-permute-start.20) | collective-permute-done | bytes 1343520 | tf_op jit(solution)/shard_map/ppermute | solution.py:37
  206.6 5.8 %finish.1 = (f32[400,1600]{1,0:T(8,128)}, f32[400,1600]{1,0:T(8,128)}) custom-call(s32[1]{0:T(128)} %bitcast.1.refs_1_.core_ref, bf16[5248,128]{1,0:T(8,128)(2,1)} %bitcast.9.own, bf16[5248,128]{1,0:T(8,128)(2,1)S(1)} %collective-permute-done.20.other, bf16[400,416]{1,0:T(8,128)(2,1)S(1)} %copy-done.4), custom_call_target="tpu_custom_call" | custom-call | bytes 19800000 | tf_op jit(solution)/shard_map/finish/pallas_call | solution.py:468
  (111 shorter events, 49.3 us)
Async XLA Ops:
  2.8 24.8 %collective-permute-start = (bf16[8,6400]{1,0:T(8,128)(2,1)S(1)}, bf16[8,6400]{1,0:T(8,128)(2,1)}, u32[]{:S(2)}, u32[]{:S(2)}) collective-permute-start(bf16[8,6400]{1,0:T(8,128)(2,1)S(1)} %edge.4.refs_0_), channel_id=1, source_target_pairs={{0,124},{4,0},{8,4},{12,8},{16,12},{20,16},{24,20},{28,24},{32,28}... | collective-permute-start | bytes 307208 | tf_op jit(solution)/shard_map/ppermute | solution.py:41
  15.1 39.4 %collective-permute-start.6 = (bf16[16,104,128]{2,1,0:T(8,128)(2,1)}, bf16[16,104,128]{2,1,0:T(8,128)(2,1)}, u32[]{:S(2)}, u32[]{:S(2)}) collective-permute-start(bf16[16,104,128]{2,1,0:T(8,128)(2,1)} %branch_share.4.refs_0_), channel_id=1, source_target_pairs={{0,2},{1,3},{2,0},{3,1},{4,6},{5,7},{6,4},{7,5},{8,10},{9,11},{10,... | collective-permute-start | bytes 1277960 | tf_op jit(solution)/shard_map/ppermute | solution.py:37
  16.6 11.0 %collective-permute-start.1 = (bf16[8,6400]{1,0:T(8,128)(2,1)}, bf16[8,6400]{1,0:T(8,128)(2,1)}, u32[]{:S(2)}, u32[]{:S(2)}) collective-permute-start(bf16[8,6400]{1,0:T(8,128)(2,1)} %edge.5.refs_0_), channel_id=1, source_target_pairs={{0,4},{4,8},{8,12},{12,16},{16,20},{20,24},{24,28},{28,32},{32,36}... | collective-permute-start | bytes 307208 | tf_op jit(solution)/shard_map/ppermute | solution.py:41
  17.8 36.7 %collective-permute-start.7 = (bf16[16,104,128]{2,1,0:T(8,128)(2,1)}, bf16[16,104,128]{2,1,0:T(8,128)(2,1)}, u32[]{:S(2)}, u32[]{:S(2)}) collective-permute-start(bf16[16,104,128]{2,1,0:T(8,128)(2,1)} %branch_share.5.refs_0_), channel_id=1, source_target_pairs={{0,3},{1,2},{2,1},{3,0},{4,7},{5,6},{6,5},{7,4},{8,11},{9,10},{10,... | collective-permute-start | bytes 1277960 | tf_op jit(solution)/shard_map/ppermute | solution.py:37
  21.2 20.4 %collective-permute-start.5 = (bf16[16,104,128]{2,1,0:T(8,128)(2,1)}, bf16[16,104,128]{2,1,0:T(8,128)(2,1)}, u32[]{:S(2)}, u32[]{:S(2)}) collective-permute-start(bf16[16,104,128]{2,1,0:T(8,128)(2,1)} %branch_share.6.refs_0_), channel_id=1, source_target_pairs={{0,1},{1,0},{2,3},{3,2},{4,5},{5,4},{6,7},{7,6},{8,9},{9,8},{10,11... | collective-permute-start | bytes 1277960 | tf_op jit(solution)/shard_map/ppermute | solution.py:37
  39.0 15.5 %collective-permute-start.2 = (bf16[16,104,128]{2,1,0:T(8,128)(2,1)}, bf16[16,104,128]{2,1,0:T(8,128)(2,1)}, u32[]{:S(2)}, u32[]{:S(2)}) collective-permute-start(bf16[16,104,128]{2,1,0:T(8,128)(2,1)} %get-tuple-element.28), channel_id=1, source_target_pairs={{0,1},{1,0},{2,3},{3,2},{4,5},{5,4},{6,7},{7,6},{8,9},{9,8},{10,11... | collective-permute-start | bytes 1277960 | tf_op jit(solution)/shard_map/ppermute | solution.py:37
  41.2 13.4 %collective-permute-start.3 = (bf16[16,104,128]{2,1,0:T(8,128)(2,1)}, bf16[16,104,128]{2,1,0:T(8,128)(2,1)}, u32[]{:S(2)}, u32[]{:S(2)}) collective-permute-start(bf16[16,104,128]{2,1,0:T(8,128)(2,1)} %get-tuple-element.29), channel_id=1, source_target_pairs={{0,2},{1,3},{2,0},{3,1},{4,6},{5,7},{6,4},{7,5},{8,10},{9,11},{10,... | collective-permute-start | bytes 1277960 | tf_op jit(solution)/shard_map/ppermute | solution.py:37
  41.6 20.5 %collective-permute-start.4 = (bf16[16,104,128]{2,1,0:T(8,128)(2,1)}, bf16[16,104,128]{2,1,0:T(8,128)(2,1)}, u32[]{:S(2)}, u32[]{:S(2)}) collective-permute-start(bf16[16,104,128]{2,1,0:T(8,128)(2,1)} %get-tuple-element.30), channel_id=1, source_target_pairs={{0,3},{1,2},{2,1},{3,0},{4,7},{5,6},{6,5},{7,4},{8,11},{9,10},{10,... | collective-permute-start | bytes 1277960 | tf_op jit(solution)/shard_map/ppermute | solution.py:37
  95.6 3.4 %collective-permute-start.8 = (bf16[5248,128]{1,0:T(8,128)(2,1)}, bf16[5248,128]{1,0:T(8,128)(2,1)S(1)}, u32[]{:S(2)}, u32[]{:S(2)}) collective-permute-start(bf16[5248,128]{1,0:T(8,128)(2,1)} %get-tuple-element.36), channel_id=1, source_target_pairs={{0,1},{1,0},{2,3},{3,2},{4,5},{5,4},{6,7},{7,6},{8,9},{9,8},{10,11... | collective-permute-start | bytes 4030472 | tf_op jit(solution)/shard_map/ppermute | solution.py:37
  101.7 44.0 %all-to-all-start = ((bf16[16,328,128]{2,1,0:T(8,128)(2,1)}), bf16[16,328,128]{2,1,0:T(8,128)(2,1)}, u32[]{:S(2)}, u32[]{:S(2)}) async-start(bf16[16,328,128]{2,1,0:T(8,128)(2,1)} %bitcast.31), calls=%async_computation | async-start | bytes 2686976 | tf_op jit(solution)/shard_map/all_to_all | solution.py:403
  106.1 3.9 %collective-permute-start.12 = (bf16[16,104,128]{2,1,0:T(8,128)(2,1)}, bf16[16,104,128]{2,1,0:T(8,128)(2,1)}, u32[]{:S(2)}, u32[]{:S(2)}) collective-permute-start(bf16[16,104,128]{2,1,0:T(8,128)(2,1)} %get-tuple-element.40), channel_id=1, source_target_pairs={{0,1},{1,0},{2,3},{3,2},{4,5},{5,4},{6,7},{7,6},{8,9},{9,8},{10,11... | collective-permute-start | bytes 1277960 | tf_op jit(solution)/shard_map/ppermute | solution.py:37
  106.5 11.5 %collective-permute-start.13 = (bf16[16,104,128]{2,1,0:T(8,128)(2,1)}, bf16[16,104,128]{2,1,0:T(8,128)(2,1)}, u32[]{:S(2)}, u32[]{:S(2)}) collective-permute-start(bf16[16,104,128]{2,1,0:T(8,128)(2,1)} %get-tuple-element.41), channel_id=1, source_target_pairs={{0,2},{1,3},{2,0},{3,1},{4,6},{5,7},{6,4},{7,5},{8,10},{9,11},{10,... | collective-permute-start | bytes 1277960 | tf_op jit(solution)/shard_map/ppermute | solution.py:37
  108.0 20.4 %collective-permute-start.14 = (bf16[16,104,128]{2,1,0:T(8,128)(2,1)}, bf16[16,104,128]{2,1,0:T(8,128)(2,1)}, u32[]{:S(2)}, u32[]{:S(2)}) collective-permute-start(bf16[16,104,128]{2,1,0:T(8,128)(2,1)} %get-tuple-element.42), channel_id=1, source_target_pairs={{0,3},{1,2},{2,1},{3,0},{4,7},{5,6},{6,5},{7,4},{8,11},{9,10},{10,... | collective-permute-start | bytes 1277960 | tf_op jit(solution)/shard_map/ppermute | solution.py:37
  108.4 28.0 %collective-permute-start.10 = (bf16[16,104,128]{2,1,0:T(8,128)(2,1)}, bf16[16,104,128]{2,1,0:T(8,128)(2,1)}, u32[]{:S(2)}, u32[]{:S(2)}) collective-permute-start(bf16[16,104,128]{2,1,0:T(8,128)(2,1)} %get-tuple-element.38), channel_id=1, source_target_pairs={{0,2},{1,3},{2,0},{3,1},{4,6},{5,7},{6,4},{7,5},{8,10},{9,11},{10,... | collective-permute-start | bytes 1277960 | tf_op jit(solution)/shard_map/ppermute | solution.py:37
  109.7 36.1 %collective-permute-start.11 = (bf16[16,104,128]{2,1,0:T(8,128)(2,1)}, bf16[16,104,128]{2,1,0:T(8,128)(2,1)}, u32[]{:S(2)}, u32[]{:S(2)}) collective-permute-start(bf16[16,104,128]{2,1,0:T(8,128)(2,1)} %get-tuple-element.39), channel_id=1, source_target_pairs={{0,3},{1,2},{2,1},{3,0},{4,7},{5,6},{6,5},{7,4},{8,11},{9,10},{10,... | collective-permute-start | bytes 1277960 | tf_op jit(solution)/shard_map/ppermute | solution.py:37
  110.1 35.7 %collective-permute-start.9 = (bf16[16,104,128]{2,1,0:T(8,128)(2,1)}, bf16[16,104,128]{2,1,0:T(8,128)(2,1)}, u32[]{:S(2)}, u32[]{:S(2)}) collective-permute-start(bf16[16,104,128]{2,1,0:T(8,128)(2,1)} %get-tuple-element.37), channel_id=1, source_target_pairs={{0,1},{1,0},{2,3},{3,2},{4,5},{5,4},{6,7},{7,6},{8,9},{9,8},{10,11... | collective-permute-start | bytes 1277960 | tf_op jit(solution)/shard_map/ppermute | solution.py:37
  147.9 5.9 %collective-permute-start.15 = (bf16[328,128]{1,0:T(8,128)(2,1)}, bf16[328,128]{1,0:T(8,128)(2,1)S(1)}, u32[]{:S(2)}, u32[]{:S(2)}) collective-permute-start(bf16[328,128]{1,0:T(8,128)(2,1)} %plane_total.1), channel_id=1, source_target_pairs={{0,64},{4,68},{8,72},{12,76},{16,80},{20,84},{24,88},{28,92},{32,9... | collective-permute-start | bytes 251912 | tf_op jit(solution)/shard_map/ppermute | solution.py:45
  150.9 3.8 %collective-permute-start.16 = (bf16[328,128]{1,0:T(8,128)(2,1)}, bf16[328,128]{1,0:T(8,128)(2,1)S(1)}, u32[]{:S(2)}, u32[]{:S(2)}) collective-permute-start(bf16[328,128]{1,0:T(8,128)(2,1)} %plane_total.1), channel_id=1, source_target_pairs={{0,2},{1,3},{2,0},{3,1},{4,6},{5,7},{6,4},{7,5},{8,10},{9,11},{10,... | collective-permute-start | bytes 251912 | tf_op jit(solution)/shard_map/ppermute | solution.py:37
  151.0 4.7 %collective-permute-start.17 = (bf16[328,128]{1,0:T(8,128)(2,1)}, bf16[328,128]{1,0:T(8,128)(2,1)S(1)}, u32[]{:S(2)}, u32[]{:S(2)}) collective-permute-start(bf16[328,128]{1,0:T(8,128)(2,1)} %plane_total.1), channel_id=1, source_target_pairs={{0,66},{1,67},{2,64},{3,65},{4,70},{5,71},{6,68},{7,69},{8,74},{9,... | collective-permute-start | bytes 251912 | tf_op jit(solution)/shard_map/ppermute | solution.py:484
  159.4 40.9 %all-to-all-start.1 = ((bf16[16,328,128]{2,1,0:T(8,128)(2,1)}), bf16[16,328,128]{2,1,0:T(8,128)(2,1)}, u32[]{:S(2)}, u32[]{:S(2)}) async-start(bf16[16,328,128]{2,1,0:T(8,128)(2,1)} %plane_copies.1), calls=%async_computation.1 | async-start | bytes 2686976 | tf_op jit(solution)/shard_map/all_to_all | solution.py:403
  169.6 15.4 %collective-permute-start.18 = (bf16[8,6656]{1,0:T(8,128)(2,1)}, bf16[8,6656]{1,0:T(8,128)(2,1)}, u32[]{:S(2)}, u32[]{:S(2)}) collective-permute-start(bf16[8,6656]{1,0:T(8,128)(2,1)} %edge.6), channel_id=1, source_target_pairs={{0,124},{4,0},{8,4},{12,8},{16,12},{20,16},{24,20},{28,24},{32,28}... | collective-permute-start | bytes 319496 | tf_op jit(solution)/shard_map/ppermute | solution.py:41
  177.0 9.5 %collective-permute-start.19 = (bf16[8,6656]{1,0:T(8,128)(2,1)S(1)}, bf16[8,6656]{1,0:T(8,128)(2,1)}, u32[]{:S(2)}, u32[]{:S(2)}) collective-permute-start(bf16[8,6656]{1,0:T(8,128)(2,1)S(1)} %edge.7), channel_id=1, source_target_pairs={{0,4},{4,8},{8,12},{12,16},{16,20},{20,24},{24,28},{28,32},{32,36}... | collective-permute-start | bytes 319496 | tf_op jit(solution)/shard_map/ppermute | solution.py:41
  189.2 17.4 %copy-start.4 = (bf16[400,416]{1,0:T(8,128)(2,1)S(1)}, bf16[400,416]{1,0:T(8,128)(2,1)}, u32[]{:S(2)}) copy-start(bf16[400,416]{1,0:T(8,128)(2,1)} %copy-done.3) | copy-start | bytes 998404
  200.3 6.3 %collective-permute-start.20 = (bf16[5248,128]{1,0:T(8,128)(2,1)}, bf16[5248,128]{1,0:T(8,128)(2,1)S(1)}, u32[]{:S(2)}, u32[]{:S(2)}) collective-permute-start(bf16[5248,128]{1,0:T(8,128)(2,1)} %bitcast.9.own), channel_id=1, source_target_pairs={{0,1},{1,0},{2,3},{3,2},{4,5},{5,4},{6,7},{7,6},{8,9},{9,8},{10,11... | collective-permute-start | bytes 4030472 | tf_op jit(solution)/shard_map/ppermute | solution.py:37
  (22 other events, 68.1 us)
